TPU v7x, 512 devices: a whole 4x8x8 slice. The times are simulated.
512 devices in a mesh: leaf: 32 (over y, x), grp: 16 (over z, core).
Axes of the slice: x: 4, y: 8, z: 8, core: 2. Of those that a mesh axis runs over, the one named last changes fastest.
Arguments:
- low_rhs: float32 [32768, 4096], P('leaf', 'grp'), may hold values from -6 to 6
- low_inverse: float32 [32768, 1024], P(('leaf', 'grp')), as said below
- panels: float32 [32768, 1024], P(('leaf', 'grp')), may hold values from -0.1875 to 0.1875
- row_blocks: int32 [32, 8], P('leaf'), may hold values from 0 to 15, all different within a row
- root_rhs: float32 [2048, 4096], P('leaf', 'grp'), may hold values from -6 to 6
- root_inverse: float32 [2048, 2048], P('leaf'), as said below
Outputs:
- low_solution: float32 [32768, 4096], P('leaf', 'grp')
- root_solution: float32 [2048, 4096], P('leaf', 'grp')
Inputs may be any that keep to these rules, and one draw needn't show every extreme that they name: `row_blocks`: each row names 8 different root blocks, and every root block is named by some row. `low_inverse`: lower triangular, with a positive diagonal. `root_inverse`: lower triangular, with a positive diagonal.
All inputs are finite; a program needn't handle non-finite values.
Results may differ from a plain program's by a relative error of at most 0.0003.
Values sent between devices are 32-bit elements; how exact they have to be, the bound alone decides.
No kernel may reach another device: no remote copies, remote signals or barrier semaphores. Data moves between devices by JAX's collectives and lax.ppermute only.
A program may use at most 64 MiB of HBM per device.

v0:
```python
import jax
import jax.numpy as jnp
from jax import lax
from jax.sharding import PartitionSpec as P

BLK = 128
NB = 16
K = 8


def body(low_rhs, low_inverse, panels, row_blocks, root_rhs, root_inverse):
    samples_dev = low_rhs.shape[1]
    low_solution = jnp.dot(
        lax.all_gather(low_inverse, "grp", axis=0, tiled=True),
        low_rhs,
        precision=lax.Precision.HIGHEST,
    )
    update = jnp.dot(
        lax.all_gather(panels, "grp", axis=0, tiled=True),
        low_solution,
        precision=lax.Precision.HIGHEST,
    )
    onehot = (row_blocks[0][None, :] == jnp.arange(NB, dtype=jnp.int32)[:, None]).astype(
        jnp.float32
    )
    placed = jnp.dot(onehot, update.reshape(K, BLK * samples_dev), precision=lax.Precision.HIGHEST)
    placed = placed.reshape(NB * BLK, samples_dev)
    gathered = lax.psum_scatter(placed, "leaf", scatter_dimension=0, tiled=True)
    root_solution = jnp.dot(
        root_inverse,
        lax.all_gather(root_rhs - gathered, "leaf", axis=0, tiled=True),
        precision=lax.Precision.HIGHEST,
    )
    return (low_solution, root_solution)


def solution(mesh):
    placed = (
        P("leaf", "grp"),
        P(("leaf", "grp"), None),
        P(("leaf", "grp"), None),
        P("leaf", None),
        P("leaf", "grp"),
        P("leaf", None),
    )
    return jax.shard_map(
        body,
        mesh=mesh,
        in_specs=placed,
        out_specs=(P("leaf", "grp"), P("leaf", "grp")),
        check_vma=False,
    )
```

profile of v0, /device:TPU:16, one launch (start us, length us, event | category | flops | bytes accessed | tf_op | source)
XLA Modules:
  0.0 436.5 jit_solution(16809426718298470623)
XLA Ops:
  7.2 0.0 copy-start
  7.2 0.0 all-gather.4.cloned.1.call-start
  7.2 0.7 all-gather.4.cloned.1.call-update
  7.9 0.0 all-gather.6.cloned.1.call-start
  8.0 0.7 all-gather.6.cloned.1.call-update
  8.7 0.0 reduce-scatter.2.cloned.1.call-start
  8.7 50.9 %all-gather.4.cloned.1.call-done = f32[1024,1024]{1,0:T(8,128)} async-done(((f32[64,1024]{1,0:T(8,128)}), f32[1024,1024]{1,0:T(8,128)}) %all-gather.4.cloned.1.call-update) | async-done | bytes 4194320 | tf_op jit(solution)/shard_map/all_gather | solution.py:14
  59.6 0.0 copy-done
  59.6 5.2 %fusion.2 = f32[1024,256]{1,0:T(8,128)S(1)} fusion(f32[1024,1024]{1,0:T(8,128)} %all-gather.4.cloned.1.call-done, f32[1024,256]{1,0:T(8,128)S(1)} %copy-done), kind=kOutput, calls=%fused_computation.5 | convolution fusion | flops 3221225472 | bytes 6291456 | tf_op jit(solution)/shard_map/dot_general | solution.py:13
  64.8 0.0 copy-start.1
  64.8 0.0 copy-start.3
  64.9 40.3 %all-gather.6.cloned.1.call-done = f32[1024,1024]{1,0:T(8,128)} async-done(((f32[64,1024]{1,0:T(8,128)}), f32[1024,1024]{1,0:T(8,128)}) %all-gather.6.cloned.1.call-update) | async-done | bytes 4194320 | tf_op jit(solution)/shard_map/all_gather | solution.py:19
  105.1 0.0 copy-done.1
  105.1 8.7 %convolution_bitcast_fusion = f32[1024,256]{0,1:T(8,128)S(1)} fusion(f32[1024,256]{1,0:T(8,128)S(1)} %fusion.2, f32[1024,1024]{1,0:T(8,128)} %all-gather.6.cloned.1.call-done), kind=kOutput, calls=%fused_computation | convolution fusion | flops 3221225472 | bytes 6291456 | tf_op jit(solution)/shard_map/dot_general | solution.py:18
  113.9 0.3 copy.8
  114.2 1.2 reshape.10
  115.4 0.0 copy-done.3
  115.4 0.0 copy-start.2
  115.4 2.2 fusion
  117.6 1.5 reshape.11
  119.1 0.0 reduce-scatter.2.cloned.1.call-update
  119.1 0.0 all-gather.8.cloned.1.call-start
  119.2 222.0 %reduce-scatter.2.cloned.1.call-done = f32[64,256]{1,0:T(8,128)} async-done(((f32[2048,256]{1,0:T(8,128)}), f32[64,256]{1,0:T(8,128)}) %reduce-scatter.2.cloned.1.call-update) | async-done | bytes 65552 | tf_op jit(solution)/shard_map/reduce_scatter | solution.py:28
  341.2 0.0 copy-done.2
  341.2 1.5 sub.3
  342.6 0.0 all-gather.8.cloned.1.call-update
  342.7 83.7 %all-gather.8.cloned.1.call-done = f32[2048,256]{1,0:T(8,128)} async-done(((f32[64,256]{1,0:T(8,128)}), f32[2048,256]{1,0:T(8,128)}) %all-gather.8.cloned.1.call-update) | async-done | bytes 2097168 | tf_op jit(solution)/shard_map/all_gather | solution.py:31
  426.3 3.6 convolution_bitcast_fusion.1
Async XLA Ops:
  7.2 52.4 %copy-start = (f32[1024,256]{1,0:T(8,128)S(1)}, f32[1024,256]{1,0:T(8,128)}, u32[]{:S(2)}) copy-start(f32[1024,256]{1,0:T(8,128)} %param.6) | copy-start | bytes 3145732
  7.2 52.4 %all-gather.4.cloned.1.call-start = ((), (), s32[]{:S(2)}) async-start(), calls=%async_computation.1 | async-start | bytes 4456448 | tf_op jit(solution)/shard_map/all_gather | solution.py:14
  7.9 97.2 %all-gather.6.cloned.1.call-start = ((), (), s32[]{:S(2)}) async-start(), calls=%async_computation.2 | async-start | bytes 4456448 | tf_op jit(solution)/shard_map/all_gather | solution.py:19
  8.7 332.5 %reduce-scatter.2.cloned.1.call-start = ((), (), s32[]{:S(2)}) async-start(), calls=%async_computation.3 | async-start | bytes 2162688 | tf_op jit(solution)/shard_map/reduce_scatter | solution.py:28
  64.8 40.3 %copy-start.1 = (f32[1024,256]{1,0:T(8,128)}, f32[1024,256]{1,0:T(8,128)S(1)}, u32[]{:S(2)}) copy-start(f32[1024,256]{1,0:T(8,128)S(1)} %fusion.2) | copy-start | bytes 3145732
  64.8 50.5 %copy-start.3 = (s32[1,8]{1,0:T(1,128)S(1)}, s32[1,8]{1,0:T(1,128)}, u32[]{:S(2)}) copy-start(s32[1,8]{1,0:T(1,128)} %param.9) | copy-start | bytes 100
  115.4 225.8 %copy-start.2 = (f32[64,256]{1,0:T(8,128)S(1)}, f32[64,256]{1,0:T(8,128)}, u32[]{:S(2)}) copy-start(f32[64,256]{1,0:T(8,128)} %param.10) | copy-start | bytes 196612
  119.1 307.2 %all-gather.8.cloned.1.call-start = ((), (), s32[]{:S(2)}) async-start(), calls=%async_computation.4 | async-start | bytes 2162688 | tf_op jit(solution)/shard_map/all_gather | solution.py:31
Sparse Core Ops, SparseCore 0:
  10.1 49.4 all-gather.3
  61.7 43.3 all-gather.5
  119.2 221.8 reduce-scatter.1
  344.8 81.5 all-gather.7
where the time goes:
time: 437 us; the launch traced here: 436 us
  waiting for transfers between devices  398 us (91%)
  matrix products  19.8 us (5%)
  between operations  13.8 us (3%)
    reduce_scatter x1, waiting for transfers between devices, body(): gathered = lax.psum_scatter(placed, 'leaf', scatter_dimension=0, tiled=True)  222 us
    all_gather x1, waiting for transfers between devices, body(): lax.all_gather(root_rhs - gathered, 'leaf', axis=0, tiled=True)  83.7 us
    all_gather x1, waiting for transfers between devices, body(): lax.all_gather(low_inverse, 'grp', axis=0, tiled=True)  50.9 us
    all_gather x1, waiting for transfers between devices, body(): lax.all_gather(panels, 'grp', axis=0, tiled=True)  40.3 us
  transfers between devices with their start and end apart: 4, of which 4 were waited for; matrix products, arithmetic and copies ran while one was open for 1% of the time, Pallas kernels for 0%

commit v1 on v0

v1 whole, which is shorter than its diff:
```python
import jax
import jax.numpy as jnp
from jax import lax
from jax.sharding import Mesh
from jax.sharding import PartitionSpec as P

BLK = 128
NB = 16
K = 8
NY, NX, NZ, NC = 8, 4, 8, 2
LEAF = ("y", "x")
GRP = ("z", "c")


def mm(a, b):
    return jnp.dot(a, b, precision=lax.Precision.HIGH, preferred_element_type=jnp.float32)


def body(low_rhs, low_inverse, panels, row_blocks, root_rhs, root_inverse):
    width = low_rhs.shape[0]
    cols = low_rhs.shape[1]
    rows = low_inverse.shape[0]
    own = root_rhs.shape[0]

    by_x = root_inverse.reshape(own, NY, NX, own).transpose(2, 0, 1, 3).reshape(NX, own, NY * own)
    root_part = lax.all_to_all(by_x, "x", 0, 0).reshape(NX * own, NY * own)

    both = lax.all_gather(jnp.concatenate([low_inverse, panels]), GRP, axis=0)
    both, root_part = lax.optimization_barrier((both, root_part))
    low_solution = mm(both[:, :rows].reshape(width, width), low_rhs)
    update = mm(both[:, rows:].reshape(width, width), low_solution)

    onehot = (row_blocks[0][None, :] == jnp.arange(NB, dtype=jnp.int32)[:, None]).astype(jnp.float32)
    placed = jnp.dot(onehot, update.reshape(K, BLK * cols), precision=lax.Precision.HIGHEST)
    parts = lax.all_to_all(placed.reshape(NY * NX, own, cols), LEAF, 0, 0)
    combined = root_rhs - jnp.sum(parts, axis=0)

    column = lax.all_to_all(jnp.broadcast_to(combined[None], (NY, own, cols)), "y", 0, 0)
    partial = mm(root_part, column.reshape(NY * own, cols))
    pieces = lax.all_to_all(partial.reshape(NX, own, cols), "x", 0, 0)
    return (low_solution, jnp.sum(pieces, axis=0))


def solution(mesh):
    fine = Mesh(mesh.devices.reshape(NY, NX, NZ, NC), LEAF + GRP)
    placed = (
        P(LEAF, GRP),
        P(LEAF + GRP, None),
        P(LEAF + GRP, None),
        P(LEAF, None),
        P(LEAF, GRP),
        P(LEAF, None),
    )
    return jax.shard_map(
        body,
        mesh=fine,
        in_specs=placed,
        out_specs=(P(LEAF, GRP), P(LEAF, GRP)),
        check_vma=False,
    )
```

time: 437 us -> 188 us (0.43)
  the two profiles are of different devices: /device:TPU:16 before, /device:TPU:2 now
where the time goes in v1:
time: 188 us
  blocking collectives  106 us (56%)
  waiting for transfers between devices  47.7 us (25%)
  between operations  14.1 us (8%)
  local copies, waits for them, and re-layouts  10.1 us (5%)
  matrix products  7.3 us (4%)
  other arithmetic  2.73 us (1%)
    all_to_all x1, blocking collectives, body(): parts = lax.all_to_all(placed.reshape(NY * NX, own, cols), LEAF, 0, 0)  60.9 us
    all_gather x1, waiting for transfers between devices, body(): both = lax.all_gather(jnp.concatenate([low_inverse, panels]), GRP, axis=0)  47.7 us
    all_to_all x1, blocking collectives, body(): lax.all_to_all(jnp.broadcast_to(combined[None], (NY, own, cols)), 'y', 0, 0)  19.3 us
    all_to_all x1, blocking collectives, body(): root_part = lax.all_to_all(by_x, 'x', 0, 0).reshape(NX * own, NY * own)  15.6 us
    all_to_all x1, blocking collectives, body(): pieces = lax.all_to_all(partial.reshape(NX, own, cols), 'x', 0, 0)  9.98 us
    dot_general x3, matrix products, mm(): jnp.dot(a, b, precision=lax.Precision.HIGH, preferred_element_type=jnp.fl...  5.12 us
    slice x1, local copies, waits for them, and re-layouts, body(): update = mm(both[:, rows:].reshape(width, width), low_solution)  4.32 us
  transfers between devices with their start and end apart: 1, of which 1 were waited for; matrix products, arithmetic and copies ran while one was open for 1% of the time, Pallas kernels for 0%

profile of v1, /device:TPU:2, one launch (start us, length us, event | category | flops | bytes accessed | tf_op | source)
XLA Modules:
  0.0 187.8 jit_solution(10933607717172281910)
XLA Ops:
  7.2 0.0 copy-start
  7.2 0.0 all-gather.3.cloned.1.call-start
  7.2 2.0 %pad_maximum_fusion = f32[128,1024]{1,0:T(8,128)} fusion(f32[64,1024]{1,0:T(8,128)} %param.8, f32[64,1024]{1,0:T(8,128)} %param.7), kind=kLoop, calls=%fused_computation.1 | loop fusion | flops 131072 | bytes 1048576 | tf_op jit(solution)/shard_map/concatenate | solution.py:28
  9.2 0.0 all-gather.3.cloned.1.call-update
  9.2 1.7 reshape.31
  10.9 0.1 copy.10
  11.0 0.3 reshape.32
  11.3 15.6 %all_to_all.20 = f32[4,64,512]{2,1,0:T(8,128)} all-to-all(f32[4,64,512]{2,1,0:T(8,128)S(1)} %reshape.32), channel_id=1, replica_groups=mesh['y'=8,'x'=4,'z'=8,'c'=2] {'x'}, dimensions={0} | all-to-all | bytes 1048576 | tf_op jit(solution)/shard_map/all_to_all | solution.py:26
  26.9 47.7 %all-gather.3.cloned.1.call-done = f32[2048,1024]{1,0:T(8,128)} async-done(((f32[128,1024]{1,0:T(8,128)}), f32[2048,1024]{1,0:T(8,128)}) %all-gather.3.cloned.1.call-update) | async-done | bytes 8388624 | tf_op jit(solution)/shard_map/all_gather | solution.py:28
  74.6 4.3 %fusion.2 = (f32[16,64,1024]{2,1,0:T(8,128)S(1)}, f32[16,64,1024]{2,1,0:T(8,128)S(1)}) fusion(f32[16,128,1024]{2,1,0:T(8,128)} %bitcast.23), kind=kLoop, calls=%fused_computation.5 | loop fusion | bytes 16777216 | tf_op jit(solution)/shard_map/slice | solution.py:31
  78.9 0.0 copy-done
  79.0 1.8 fusion.3
  80.8 0.0 copy-start.1
  80.8 1.0 copy-done.1
  81.8 0.0 copy-start.3
  81.8 1.8 fusion.4
  83.6 1.2 reshape.36
  84.8 0.0 copy-done.3
  84.8 2.2 %fusion = f32[16,32768]{1,0:T(8,128)S(1)} fusion(f32[8,32768]{1,0:T(8,128)} %reshape.36, s32[8]{0:T(128)S(1)} %bitcast.26), kind=kOutput, calls=%fused_computation.3 | convolution fusion | flops 50331776 | bytes 3145760 | tf_op jit(solution)/shard_map/dot_general | solution.py:34
  87.0 1.5 reshape.37
  88.5 0.0 copy-start.2
  88.5 60.9 %all_to_all.21 = f32[32,64,256]{2,1,0:T(8,128)S(1)} all-to-all(f32[32,64,256]{2,1,0:T(8,128)} %reshape.37), channel_id=1, replica_groups=mesh['y'=8,'x'=4,'z'=8,'c'=2] {'y','x'}, dimensions={0} | all-to-all | bytes 4194304 | tf_op jit(solution)/shard_map/all_to_all | solution.py:35
  149.4 0.1 reduce_sum.18
  149.6 0.0 copy-done.2
  149.6 19.3 %all_to_all.22 = f32[8,64,256]{2,1,0:T(8,128)S(1)} all-to-all(f32[8,64,256]{2,1,0:T(8,128)S(1)} %broadcast_in_dim.2), channel_id=1, replica_groups=mesh['y'=8,'x'=4,'z'=8,'c'=2] {'y'}, dimensions={0} | all-to-all | bytes 1048576 | tf_op jit(solution)/shard_map/all_to_all | solution.py:38
  168.9 1.4 fusion.5
  170.4 10.0 %all_to_all.23 = f32[4,64,256]{2,1,0:T(8,128)S(1)} all-to-all(f32[4,64,256]{2,1,0:T(8,128)S(1)} %fusion.5), channel_id=1, replica_groups=mesh['y'=8,'x'=4,'z'=8,'c'=2] {'x'}, dimensions={0} | all-to-all | bytes 524288 | tf_op jit(solution)/shard_map/all_to_all | solution.py:40
  180.4 0.6 reduce_sum.19
  (2 shorter events, 0.0 us)
Async XLA Ops:
  7.2 71.8 %copy-start = (f32[1024,256]{1,0:T(8,128)S(1)}, f32[1024,256]{1,0:T(8,128)}, u32[]{:S(2)}) copy-start(f32[1024,256]{1,0:T(8,128)} %param.6) | copy-start | bytes 3145732
  7.2 67.4 %all-gather.3.cloned.1.call-start = ((), (), s32[]{:S(2)}) async-start(), calls=%async_computation.4 | async-start | bytes 8912896 | tf_op jit(solution)/shard_map/all_gather | solution.py:28
  80.8 1.0 copy-start.1
  81.8 3.0 %copy-start.3 = (s32[1,8]{1,0:T(1,128)S(1)}, s32[1,8]{1,0:T(1,128)}, u32[]{:S(2)}) copy-start(s32[1,8]{1,0:T(1,128)} %param.9) | copy-start | bytes 100
  88.5 61.1 %copy-start.2 = (f32[64,256]{1,0:T(8,128)S(1)}, f32[64,256]{1,0:T(8,128)}, u32[]{:S(2)}) copy-start(f32[64,256]{1,0:T(8,128)} %param.10) | copy-start | bytes 196612
Sparse Core Ops, SparseCore 0:
  10.7 63.9 all-gather.2

commit v2 on v1

v2 whole, which is shorter than its diff:
```python
import jax
import jax.numpy as jnp
from jax import lax
from jax.experimental import pallas as pl
from jax.experimental.pallas import tpu as pltpu
from jax.sharding import Mesh
from jax.sharding import PartitionSpec as P

BLK = 128
NB = 16
K = 8
NY, NX, NZ, NC = 8, 4, 8, 2
LEAF = ("y", "x")
GRP = ("z", "c")
SUB, LANE = 8, 128
VMEM = pl.BlockSpec(memory_space=pltpu.VMEM)
SMEM = pl.BlockSpec(memory_space=pltpu.SMEM)


def split(a):
    hi = a.astype(jnp.bfloat16)
    return hi, (a - hi.astype(jnp.float32)).astype(jnp.bfloat16)


def dot3(a, b_hi, b_lo):
    hi, lo = split(a)
    d = lambda u, v: jnp.dot(u, v, preferred_element_type=jnp.float32)
    return d(hi, b_hi) + (d(hi, b_lo) + d(lo, b_hi))


def solve_kernel(both_ref, rhs_ref, low_ref, tiles_ref, r_hi, r_lo, s_hi, s_lo):
    step = pl.program_id(0)
    rows = both_ref.shape[0] * both_ref.shape[1]

    @pl.when(step == 0)
    def _():
        r_hi[...], r_lo[...] = split(rhs_ref[...])

    for i in range(4):

        @pl.when(step == i)
        def _():
            deep = (i + 1) * rows
            a = both_ref[...].reshape(rows, both_ref.shape[2])[:, :deep]
            s = dot3(a, r_hi[:deep], r_lo[:deep])
            here = pl.ds(i * rows, rows)
            low_ref[here, :] = s
            s_hi[here, :], s_lo[here, :] = split(s)

    for i in range(4):

        @pl.when(step == 4 + i)
        def _():
            u = dot3(both_ref[...].reshape(rows, both_ref.shape[2]), s_hi[...], s_lo[...])
            for half in range(2):
                k = 2 * i + half
                for y in range(NY):
                    for x in range(NX):
                        r = BLK * half + SUB * (NY * (x % 2) + y)
                        c = LANE * (x // 2)
                        tiles_ref[NX * y + x, SUB * k : SUB * (k + 1), :] = u[r : r + SUB, c : c + LANE]


def solve(both, rhs):
    shards, rows2, width = both.shape
    rows, cols = rows2 // 2, rhs.shape[1]
    return pl.pallas_call(
        solve_kernel,
        grid=(8,),
        in_specs=[
            pl.BlockSpec((shards // 4, rows, width), lambda i: (i % 4, i // 4, 0)),
            pl.BlockSpec((width, cols), lambda i: (0, 0)),
        ],
        out_specs=[
            pl.BlockSpec((width, cols), lambda i: (0, 0)),
            pl.BlockSpec((NY * NX, K * SUB, LANE), lambda i: (0, 0, 0)),
        ],
        out_shape=[
            jax.ShapeDtypeStruct((width, cols), jnp.float32),
            jax.ShapeDtypeStruct((NY * NX, K * SUB, LANE), jnp.float32),
        ],
        scratch_shapes=[pltpu.VMEM((width, cols), jnp.bfloat16)] * 4,
        name="solve",
    )(both, rhs)


def collect_kernel(index_ref, start_ref, parts_ref, out_ref, acc):
    acc[...] = start_ref[...]

    def one(s, carry):
        at = [pl.multiple_of(index_ref[s, k] * SUB, SUB) for k in range(K)]
        new = [acc[pl.ds(at[k], SUB), :] - parts_ref[s, SUB * k : SUB * (k + 1), :] for k in range(K)]
        for k in range(K):
            acc[pl.ds(at[k], SUB), :] = new[k]
        return carry

    lax.fori_loop(0, parts_ref.shape[0], one, 0)
    for y in range(NY):
        out_ref[y] = acc[...]


def collect(index, start, parts):
    return pl.pallas_call(
        collect_kernel,
        in_specs=[SMEM, VMEM, VMEM],
        out_specs=VMEM,
        out_shape=jax.ShapeDtypeStruct((NY, NB * SUB, LANE), jnp.float32),
        scratch_shapes=[pltpu.VMEM((NB * SUB, LANE), jnp.float32)],
        name="collect",
    )(index, start, parts)


def root_kernel(inv_ref, column_ref, out_ref):
    tiles = [column_ref[y, SUB * b : SUB * (b + 1), :] for b in range(NB) for y in range(NY)]
    hi, lo = split(jnp.concatenate(tiles))
    out = dot3(inv_ref[...].reshape(-1, inv_ref.shape[2]), hi, lo)
    out_ref[...] = out.reshape(out_ref.shape)


def root(inv, column):
    return pl.pallas_call(
        root_kernel,
        in_specs=[VMEM, VMEM],
        out_specs=VMEM,
        out_shape=jax.ShapeDtypeStruct((inv.shape[0], inv.shape[1], LANE), jnp.float32),
        name="root",
    )(inv, column)


def body(low_rhs, low_inverse, panels, row_blocks, root_rhs, root_inverse):
    own = root_rhs.shape[0]
    parity = lax.axis_index("x") % 2

    by_parity = root_inverse.reshape(own, NB, 2, BLK // 2).transpose(2, 0, 1, 3).reshape(2, own, NB * BLK // 2)
    inv = lax.all_to_all(jnp.concatenate([by_parity, by_parity]), "x", 0, 0)
    rhs_tiles = root_rhs.reshape(NY, 1, SUB, 2, 1, LANE).transpose(0, 3, 4, 1, 2, 5)
    rhs_tiles = jnp.broadcast_to(rhs_tiles.reshape(NY, 2, 1, SUB, LANE), (NY, 2, 2, SUB, LANE))
    blocks = jnp.pad(row_blocks.astype(jnp.float32), ((0, SUB - 1), (0, LANE - K)))
    early = jnp.concatenate(
        [rhs_tiles.reshape(NY * NX, SUB, LANE), jnp.broadcast_to(blocks[None], (NY * NX, SUB, LANE))], axis=1
    )
    early = lax.all_to_all(early, LEAF, 0, 0)
    index = early[:, SUB, :K].astype(jnp.int32)
    start = lax.dynamic_index_in_dim(early[:, :SUB].reshape(NB, 2, SUB, LANE), parity, 1, keepdims=False)
    start = start.reshape(NB * SUB, LANE)

    both = lax.all_gather(jnp.concatenate([low_inverse, panels]), GRP, axis=0)
    both, inv, index, start = lax.optimization_barrier((both, inv, index, start))

    low_solution, tiles = solve(both, low_rhs)
    parts = lax.all_to_all(tiles, LEAF, 0, 0)
    column = lax.all_to_all(collect(index, start, parts), "y", 0, 0)
    pieces = lax.all_to_all(root(inv, column), "x", 0, 0)
    return (low_solution, jnp.concatenate([pieces[0] + pieces[1], pieces[2] + pieces[3]], axis=1))


def solution(mesh):
    fine = Mesh(mesh.devices.reshape(NY, NX, NZ, NC), LEAF + GRP)
    placed = (
        P(LEAF, GRP),
        P(LEAF + GRP, None),
        P(LEAF + GRP, None),
        P(LEAF, None),
        P(LEAF, GRP),
        P(LEAF, None),
    )
    return jax.shard_map(
        body,
        mesh=fine,
        in_specs=placed,
        out_specs=(P(LEAF, GRP), P(LEAF, GRP)),
        check_vma=False,
    )
```

time: 188 us -> 166 us (0.88)
  blocking collectives: 106 us -> 68.9 us
  starting transfers between devices: 0.04 us -> 15.6 us
  Pallas kernels: 0 us -> 14.8 us
  matrix products: 7.3 us -> 0 us
  local copies, waits for them, and re-layouts: 10.1 us -> 3.73 us
  waiting for transfers between devices: 47.7 us -> 42.5 us
  other arithmetic: 2.73 us -> 5.64 us
    all_to_all x4 -> x3, blocking collectives: 106 us -> 68.9 us  [the longest x1 38.4 us: body(): parts = lax.all_to_all(tiles, LEAF, 0, 0)]
    all_gather x1, waiting for transfers between devices: 47.7 us -> 23.7 us  [body(): both = lax.all_gather(jnp.concatenate([low_inverse, panels]), GRP, axis=0)]
    all_to_all x0 -> x2, waiting for transfers between devices: none -> 18.8 us  [the longest x1 10.9 us: body(): inv = lax.all_to_all(jnp.concatenate([by_parity, by_parity]), 'x', 0, 0)]
    all_to_all x0 -> x2, starting transfers between devices: none -> 15.6 us  [the longest x1 10.3 us: body(): early = lax.all_to_all(early, LEAF, 0, 0)]
    pallas_call x0 -> x3, Pallas kernels: none -> 14.8 us  [the longest x1 9.61 us: solve(): pl.pallas_call(solve_kernel, grid=(8,), in_specs=[pl.BlockSpec((shards //...]
    dot_general x4 -> x0, matrix products: 7.3 us -> none  [the longest x3 5.12 us: mm(): jnp.dot(a, b, precision=lax.Precision.HIGH, preferred_element_type=jnp.fl...]
    slice x1 -> x2, local copies, waits for them, and re-layouts: 4.32 us -> 0.02 us  [the longest x1 0.01 us: body(): early[:, :SUB].reshape(NB, 2, SUB, LANE)]
    concatenate x0 -> x3, other arithmetic: none -> 2.49 us  [the longest x1 1.1 us: body(): inv = lax.all_to_all(jnp.concatenate([by_parity, by_parity]), 'x', 0, 0)]
  transfers between devices with their start and end apart: 1 -> 3, of which waited for: 1 -> 3; matrix products, arithmetic and copies ran while one was open for 1% -> 4% of each run, Pallas kernels for 0% -> 0%
where the time goes in v2:
time: 166 us; the launch traced here: 165 us
  blocking collectives  68.9 us (42%)
  waiting for transfers between devices  42.5 us (26%)
  starting transfers between devices  15.6 us (9%)
  Pallas kernels  14.8 us (9%)
  between operations  14.1 us (8%)
  other arithmetic  5.64 us (3%)
  local copies, waits for them, and re-layouts  3.73 us (2%)
    all_to_all x1, blocking collectives, body(): parts = lax.all_to_all(tiles, LEAF, 0, 0)  38.4 us
    all_gather x1, waiting for transfers between devices, body(): both = lax.all_gather(jnp.concatenate([low_inverse, panels]), GRP, axis=0)  23.7 us
    all_to_all x1, blocking collectives, body(): column = lax.all_to_all(collect(index, start, parts), 'y', 0, 0)  20.3 us
    all_to_all x1, waiting for transfers between devices, body(): inv = lax.all_to_all(jnp.concatenate([by_parity, by_parity]), 'x', 0, 0)  10.9 us
    all_to_all x1, starting transfers between devices, body(): early = lax.all_to_all(early, LEAF, 0, 0)  10.3 us
    all_to_all x1, blocking collectives, body(): pieces = lax.all_to_all(root(inv, column), 'x', 0, 0)  10.2 us
    pallas_call x1, Pallas kernels, solve(): pl.pallas_call(solve_kernel, grid=(8,), in_specs=[pl.BlockSpec((shards //...  9.61 us
    all_to_all x1, waiting for transfers between devices, body(): early = lax.all_to_all(early, LEAF, 0, 0)  7.9 us
  transfers between devices with their start and end apart: 3, of which 3 were waited for; matrix products, arithmetic and copies ran while one was open for 4% of the time, Pallas kernels for 0%

profile of v2, /device:TPU:2, one launch (start us, length us, event | category | flops | bytes accessed | tf_op | source)
XLA Modules:
  0.0 165.3 jit_solution(12555661387083235475)
XLA Ops:
  7.2 0.0 all-gather.3.cloned.1.call-start
  7.2 1.9 %pad_maximum_fusion.1 = f32[128,1024]{1,0:T(8,128)} fusion(f32[64,1024]{1,0:T(8,128)} %param.8, f32[64,1024]{1,0:T(8,128)} %param.7), kind=kLoop, calls=%fused_computation.2 | loop fusion | flops 131072 | bytes 1048576 | tf_op jit(solution)/shard_map/concatenate | solution.py:147
  9.1 0.0 all-gather.3.cloned.1.call-update
  9.1 0.7 convert_element_type.11
  9.8 0.8 broadcast_in_dim.14
  10.6 0.8 pad_maximum_fusion.2
  11.4 10.3 %all-to-all-start.1 = ((f32[32,16,128]{2,1,0:T(8,128)}), f32[32,16,128]{2,1,0:T(8,128)S(1)}, u32[]{:S(2)}, u32[]{:S(2)}) async-start(f32[32,16,128]{2,1,0:T(8,128)} %pad_maximum_fusion.2), calls=%async_computation.1 | async-start | bytes 524288 | tf_op jit(solution)/shard_map/all_to_all | solution.py:142
  21.7 1.8 %reshape.29 = f32[64,16,2,64]{3,2,1,0:T(2,128)S(1)} reshape(f32[64,2048]{1,0:T(8,128)} %param.11) | data formatting | bytes 1048576 | tf_op jit(solution)/shard_map/reshape | solution.py:134
  23.5 0.1 copy.17
  23.6 0.3 reshape.30
  23.9 1.1 pad_maximum_fusion
  25.0 7.9 %all-to-all-done.1 = f32[32,16,128]{2,1,0:T(8,128)S(1)} async-done(((f32[32,16,128]{2,1,0:T(8,128)}), f32[32,16,128]{2,1,0:T(8,128)S(1)}, u32[]{:S(2)}, u32[]{:S(2)}) %all-to-all-start.1) | async-done | bytes 262176 | tf_op jit(solution)/shard_map/all_to_all | solution.py:142
  32.9 5.3 %all-to-all-start = ((f32[4,64,1024]{2,1,0:T(8,128)}), f32[4,64,1024]{2,1,0:T(8,128)S(1)}, u32[]{:S(2)}, u32[]{:S(2)}) async-start(f32[4,64,1024]{2,1,0:T(8,128)} %pad_maximum_fusion), calls=%async_computation | async-start | bytes 2097152 | tf_op jit(solution)/shard_map/all_to_all | solution.py:135
  38.2 0.6 dynamic-slice_bitcast_fusion.start_ref
  38.9 0.6 convert_bitcast_fusion.index_ref
  39.5 10.9 %all-to-all-done.inv_ref = f32[4,64,1024]{2,1,0:T(8,128)S(1)} async-done(((f32[4,64,1024]{2,1,0:T(8,128)}), f32[4,64,1024]{2,1,0:T(8,128)S(1)}, u32[]{:S(2)}, u32[]{:S(2)}) %all-to-all-start) | async-done | bytes 1048608 | tf_op jit(solution)/shard_map/all_to_all | solution.py:135
  50.3 0.0 copy-start
  50.3 23.7 %all-gather.3.cloned.1.call-done = f32[2048,1024]{1,0:T(8,128)} async-done(((f32[128,1024]{1,0:T(8,128)}), f32[2048,1024]{1,0:T(8,128)}) %all-gather.3.cloned.1.call-update) | async-done | bytes 8388624 | tf_op jit(solution)/shard_map/all_gather | solution.py:147
  74.0 9.6 %solve.1 = (f32[1024,256]{1,0:T(8,128)}, f32[32,64,128]{2,1,0:T(8,128)}) custom-call(f32[16,128,1024]{2,1,0:T(8,128)} %bitcast.24, f32[1024,256]{1,0:T(8,128)} %rhs_ref.1), custom_call_target="tpu_custom_call" | custom-call | tf_op jit(solution)/shard_map/solve/pallas_call | solution.py:67
  83.7 38.4 %all_to_all.25.parts_ref = f32[32,64,128]{2,1,0:T(8,128)} all-to-all(f32[32,64,128]{2,1,0:T(8,128)} %get-tuple-element.13), channel_id=1, replica_groups=mesh['y'=8,'x'=4,'z'=8,'c'=2] {'y','x'}, dimensions={0} | all-to-all | bytes 2097152 | tf_op jit(solution)/shard_map/all_to_all | solution.py:151
  122.1 2.6 %collect.1 = f32[8,128,128]{2,1,0:T(8,128)} custom-call(s32[32,8]{1,0:T(8,128)} %convert_bitcast_fusion.index_ref, f32[128,128]{1,0:T(8,128)} %dynamic-slice_bitcast_fusion.start_ref, f32[32,64,128]{2,1,0:T(8,128)} %all_to_all.25.parts_ref), custom_call_target="tpu_custom_call" | custom-call | tf_op jit(solution)/shard_map/collect/pallas_call | solution.py:103
  124.7 20.3 %all_to_all.26.column_ref = f32[8,128,128]{2,1,0:T(8,128)} all-to-all(f32[8,128,128]{2,1,0:T(8,128)} %collect.1), channel_id=1, replica_groups=mesh['y'=8,'x'=4,'z'=8,'c'=2] {'y'}, dimensions={0} | all-to-all | bytes 1048576 | tf_op jit(solution)/shard_map/all_to_all | solution.py:152
  145.0 0.0 copy-done
  145.0 2.6 %root.1 = f32[4,64,128]{2,1,0:T(8,128)} custom-call(f32[4,64,1024]{2,1,0:T(8,128)} %copy-done, f32[8,128,128]{2,1,0:T(8,128)} %all_to_all.26.column_ref), custom_call_target="tpu_custom_call" | custom-call | tf_op jit(solution)/shard_map/root/pallas_call | solution.py:121
  147.6 10.2 %all_to_all.27 = f32[4,64,128]{2,1,0:T(8,128)S(1)} all-to-all(f32[4,64,128]{2,1,0:T(8,128)} %root.1), channel_id=1, replica_groups=mesh['y'=8,'x'=4,'z'=8,'c'=2] {'x'}, dimensions={0} | all-to-all | bytes 262144 | tf_op jit(solution)/shard_map/all_to_all | solution.py:153
  157.8 0.6 pad_maximum_fusion.3
  (5 shorter events, 0.0 us)
Async XLA Ops:
  7.2 66.9 %all-gather.3.cloned.1.call-start = ((), (), s32[]{:S(2)}) async-start(), calls=%async_computation.5 | async-start | bytes 8912896 | tf_op jit(solution)/shard_map/all_gather | solution.py:147
  11.4 21.5 %all-to-all-start.1 = ((f32[32,16,128]{2,1,0:T(8,128)}), f32[32,16,128]{2,1,0:T(8,128)S(1)}, u32[]{:S(2)}, u32[]{:S(2)}) async-start(f32[32,16,128]{2,1,0:T(8,128)} %pad_maximum_fusion.2), calls=%async_computation.1 | async-start | bytes 524288 | tf_op jit(solution)/shard_map/all_to_all | solution.py:142
  32.9 17.5 %all-to-all-start = ((f32[4,64,1024]{2,1,0:T(8,128)}), f32[4,64,1024]{2,1,0:T(8,128)S(1)}, u32[]{:S(2)}, u32[]{:S(2)}) async-start(f32[4,64,1024]{2,1,0:T(8,128)} %pad_maximum_fusion), calls=%async_computation | async-start | bytes 2097152 | tf_op jit(solution)/shard_map/all_to_all | solution.py:135
  50.3 94.7 %copy-start = (f32[4,64,1024]{2,1,0:T(8,128)}, f32[4,64,1024]{2,1,0:T(8,128)S(1)}, u32[]{:S(2)}) copy-start(f32[4,64,1024]{2,1,0:T(8,128)S(1)} %all-to-all-done.inv_ref) | copy-start | bytes 3145732
Sparse Core Ops, SparseCore 0:
  10.1 63.9 all-gather.2

commit v3 on v2

v3 whole, which is shorter than its diff:
```python
import jax
import jax.numpy as jnp
from jax import lax
from jax.experimental import pallas as pl
from jax.experimental.pallas import tpu as pltpu
from jax.sharding import Mesh
from jax.sharding import PartitionSpec as P

BLK = 128
NB = 16
K = 8
NY, NX, NZ, NC = 8, 4, 8, 2
LEAF = ("y", "x")
GRP = ("z", "c")
SUB, LANE = 8, 128
VMEM = pl.BlockSpec(memory_space=pltpu.VMEM)
SMEM = pl.BlockSpec(memory_space=pltpu.SMEM)


def split(a):
    hi = a.astype(jnp.bfloat16)
    return hi, (a - hi.astype(jnp.float32)).astype(jnp.bfloat16)


def dot3(a, b_hi, b_lo):
    hi, lo = split(a)
    d = lambda u, v: jnp.dot(u, v, preferred_element_type=jnp.float32)
    return d(hi, b_hi) + (d(hi, b_lo) + d(lo, b_hi))


def solve_kernel(both_ref, rhs_ref, low_ref, tiles_ref, l_buf, p_buf, s_hi, s_lo, sems):
    parts, shards, rows, width = l_buf.shape
    part = shards * rows

    def read(i):
        here = pl.ds(shards * (i % parts), shards)
        if i < parts:
            deep = pl.ds(0, (i + 1) * part)
            src, dst = both_ref.at[here, pl.ds(0, rows), deep], l_buf.at[i, :, :, deep]
        else:
            src, dst = both_ref.at[here, pl.ds(rows, rows), :], p_buf.at[i - parts]
        return pltpu.make_async_copy(src, dst, sems.at[i])

    reads = [read(i) for i in range(2 * parts)]
    for copy in reads:
        copy.start()
    r_hi, r_lo = split(rhs_ref[...])
    for i in range(parts):
        reads[i].wait()
        deep = (i + 1) * part
        s = dot3(l_buf[i].reshape(part, width)[:, :deep], r_hi[:deep], r_lo[:deep])
        here = pl.ds(i * part, part)
        low_ref[here, :] = s
        s_hi[here, :], s_lo[here, :] = split(s)
    for i in range(parts):
        reads[parts + i].wait()
        u = dot3(p_buf[i].reshape(part, width), s_hi[...], s_lo[...])
        for j in range(part // BLK):
            k = i * (part // BLK) + j
            for y in range(NY):
                for x in range(NX):
                    r = BLK * j + SUB * (NX * (y // 2) + x)
                    c = LANE * (y % 2)
                    tiles_ref[NX * y + x, SUB * k : SUB * (k + 1), :] = u[r : r + SUB, c : c + LANE]


def solve(both, rhs, parts=2):
    shards, rows2, width = both.shape
    rows, cols = rows2 // 2, rhs.shape[1]
    return pl.pallas_call(
        solve_kernel,
        in_specs=[pl.BlockSpec(memory_space=pltpu.HBM), VMEM],
        out_specs=[VMEM, VMEM],
        out_shape=[
            jax.ShapeDtypeStruct((width, cols), jnp.float32),
            jax.ShapeDtypeStruct((NY * NX, K * SUB, LANE), jnp.float32),
        ],
        scratch_shapes=[pltpu.VMEM((parts, shards // parts, rows, width), jnp.float32)] * 2
        + [pltpu.VMEM((width, cols), jnp.bfloat16)] * 2
        + [pltpu.SemaphoreType.DMA((2 * parts,))],
        compiler_params=pltpu.CompilerParams(vmem_limit_bytes=28 << 20),
        name="solve",
    )(both, rhs)


def collect_kernel(index_ref, start_ref, parts_ref, out_ref, acc):
    acc[...] = start_ref[...]

    def one(s, carry):
        at = [pl.multiple_of(index_ref[s, k] * SUB, SUB) for k in range(K)]
        new = [acc[pl.ds(at[k], SUB), :] - parts_ref[s, SUB * k : SUB * (k + 1), :] for k in range(K)]
        for k in range(K):
            acc[pl.ds(at[k], SUB), :] = new[k]
        return carry

    lax.fori_loop(0, parts_ref.shape[0], one, 0)
    for x in range(NX):
        out_ref[x] = acc[...]


def collect(index, start, parts):
    return pl.pallas_call(
        collect_kernel,
        in_specs=[SMEM, VMEM, VMEM],
        out_specs=VMEM,
        out_shape=jax.ShapeDtypeStruct((NX, NB * SUB, LANE), jnp.float32),
        scratch_shapes=[pltpu.VMEM((NB * SUB, LANE), jnp.float32)],
        compiler_params=pltpu.CompilerParams(vmem_limit_bytes=12 << 20),
        name="collect",
    )(index, start, parts)


def root_kernel(inv_ref, column_ref, out_ref):
    tiles = [column_ref[x, SUB * b : SUB * (b + 1), :] for b in range(NB) for x in range(NX)]
    hi, lo = split(jnp.concatenate(tiles))
    out = dot3(inv_ref[...].reshape(-1, inv_ref.shape[2]), hi, lo)
    out_ref[...] = out.reshape(out_ref.shape)


def root(inv, column):
    return pl.pallas_call(
        root_kernel,
        in_specs=[VMEM, VMEM],
        out_specs=VMEM,
        out_shape=jax.ShapeDtypeStruct((inv.shape[0], inv.shape[1], LANE), jnp.float32),
        compiler_params=pltpu.CompilerParams(vmem_limit_bytes=12 << 20),
        name="root",
    )(inv, column)


def body(low_rhs, low_inverse, panels, row_blocks, root_rhs, root_inverse):
    own = root_rhs.shape[0]
    y = lax.axis_index("y")

    some = BLK // 4
    by_y = root_inverse.reshape(own, NB, 4, some).transpose(2, 0, 1, 3).reshape(4, 1, own, NB * some)
    inv = lax.all_to_all(jnp.broadcast_to(by_y, (4, 2, own, NB * some)).reshape(NY, own, NB * some), "y", 0, 0)
    rhs_tiles = root_rhs.reshape(2, NX, SUB, 2, LANE).transpose(0, 3, 1, 2, 4)
    rhs_tiles = jnp.broadcast_to(rhs_tiles[None], (2, 2, 2, NX, SUB, LANE))
    blocks = jnp.pad(row_blocks.astype(jnp.float32), ((0, SUB - 1), (0, LANE - K)))
    early = jnp.concatenate(
        [rhs_tiles.reshape(NY * NX, SUB, LANE), jnp.broadcast_to(blocks[None], (NY * NX, SUB, LANE))], axis=1
    )
    early = lax.all_to_all(early, LEAF, 0, 0)
    index = early[:, SUB, :K].astype(jnp.int32)
    start = lax.dynamic_index_in_dim(early[:, :SUB].reshape(NB, 2, SUB, LANE), y // 4, 1, keepdims=False)
    start = start.reshape(NB * SUB, LANE)

    both = lax.all_gather(jnp.concatenate([low_inverse, panels]), GRP, axis=0)
    both, inv, index, start = lax.optimization_barrier((both, inv, index, start))

    low_solution, tiles = solve(both, low_rhs)
    parts = lax.all_to_all(tiles, LEAF, 0, 0)
    column = lax.all_to_all(collect(index, start, parts), "x", 0, 0)
    pieces = lax.all_to_all(root(inv, column), "y", 0, 0)
    halves = jnp.sum(pieces.reshape(4, 2, own, LANE), axis=0)
    return (low_solution, jnp.concatenate([halves[0], halves[1]], axis=1))


def solution(mesh):
    fine = Mesh(mesh.devices.reshape(NY, NX, NZ, NC), LEAF + GRP)
    placed = (
        P(LEAF, GRP),
        P(LEAF + GRP, None),
        P(LEAF + GRP, None),
        P(LEAF, None),
        P(LEAF, GRP),
        P(LEAF, None),
    )
    return jax.shard_map(
        body,
        mesh=fine,
        in_specs=placed,
        out_specs=(P(LEAF, GRP), P(LEAF, GRP)),
        check_vma=False,
    )
```

time: 166 us -> 155 us (0.934)
  blocking collectives: 68.9 us -> 60.8 us
  Pallas kernels: 14.8 us -> 8.68 us
  local copies, waits for them, and re-layouts: 3.73 us -> 7.18 us
  waiting for transfers between devices: 42.5 us -> 45.7 us
  starting transfers between devices: 15.6 us -> 13.8 us
    all_to_all x1, waiting for transfers between devices: 10.9 us -> 27.4 us  [body(): lax.all_to_all(jnp.broadcast_to(by_y, (4, 2, own, NB * some)).reshape(NY,...]
    all_gather x1, waiting for transfers between devices: 23.7 us -> 8.95 us  [body(): both = lax.all_gather(jnp.concatenate([low_inverse, panels]), GRP, axis=0)]
    all_to_all x2, blocking collectives: 30.5 us -> 22.7 us  [the longest x1 12.9 us: body(): pieces = lax.all_to_all(root(inv, column), 'y', 0, 0)]
    unnamed x2 -> x5, local copies, waits for them, and re-layouts: 0.01 us -> 4.76 us
    pallas_call x1, Pallas kernels: 9.61 us -> 6.78 us  [solve(): pl.pallas_call(solve_kernel, in_specs=[pl.BlockSpec(memory_space=pltpu.HB...]
    reshape x3 -> x0, local copies, waits for them, and re-layouts: 2.19 us -> none  [body(): root_inverse.reshape(own, NB, 2, BLK // 2).transpose(2, 0, 1, 3)]
    pallas_call x1, Pallas kernels: 2.58 us -> 0.58 us  [root(): pl.pallas_call(root_kernel, in_specs=[VMEM, VMEM], out_specs=VMEM, out_sh...]
    all_to_all x1, starting transfers between devices: 5.32 us -> 3.56 us  [body(): lax.all_to_all(jnp.broadcast_to(by_y, (4, 2, own, NB * some)).reshape(NY,...]
  transfers between devices with their start and end apart: 3 -> 3, of which waited for: 3 -> 3; matrix products, arithmetic and copies ran while one was open for 4% -> 3% of each run, Pallas kernels for 0% -> 0%
where the time goes in v3:
time: 155 us; the launch traced here: 154 us
  blocking collectives  60.8 us (39%)
  waiting for transfers between devices  45.7 us (29%)
  between operations  14.2 us (9%)
  starting transfers between devices  13.8 us (9%)
  Pallas kernels  8.68 us (6%)
  local copies, waits for them, and re-layouts  7.18 us (5%)
  other arithmetic  4.03 us (3%)
    all_to_all x1, blocking collectives, body(): parts = lax.all_to_all(tiles, LEAF, 0, 0)  38.1 us
    all_to_all x1, waiting for transfers between devices, body(): lax.all_to_all(jnp.broadcast_to(by_y, (4, 2, own, NB * some)).reshape(NY,...  27.4 us
    all_to_all x1, blocking collectives, body(): pieces = lax.all_to_all(root(inv, column), 'y', 0, 0)  12.9 us
    all_to_all x1, starting transfers between devices, body(): early = lax.all_to_all(early, LEAF, 0, 0)  10.2 us
    all_to_all x1, blocking collectives, body(): column = lax.all_to_all(collect(index, start, parts), 'x', 0, 0)  9.82 us
    all_to_all x1, waiting for transfers between devices, body(): early = lax.all_to_all(early, LEAF, 0, 0)  9.42 us
    all_gather x1, waiting for transfers between devices, body(): both = lax.all_gather(jnp.concatenate([low_inverse, panels]), GRP, axis=0)  8.95 us
    pallas_call x1, Pallas kernels, solve(): pl.pallas_call(solve_kernel, in_specs=[pl.BlockSpec(memory_space=pltpu.HB...  6.78 us
  transfers between devices with their start and end apart: 3, of which 3 were waited for; matrix products, arithmetic and copies ran while one was open for 3% of the time, Pallas kernels for 0%

profile of v3, /device:TPU:2, one launch (start us, length us, event | category | flops | bytes accessed | tf_op | source)
XLA Modules:
  0.0 154.5 jit_solution(13205843729090757998)
XLA Ops:
  7.2 0.0 copy-start.1
  7.2 0.0 all-gather.3.cloned.1.call-start
  7.2 2.0 %pad_maximum_fusion = f32[128,1024]{1,0:T(8,128)} fusion(f32[64,1024]{1,0:T(8,128)} %param.8, f32[64,1024]{1,0:T(8,128)} %param.7), kind=kLoop, calls=%fused_computation | loop fusion | flops 131072 | bytes 1048576 | tf_op jit(solution)/shard_map/concatenate | solution.py:149
  9.2 0.0 all-gather.3.cloned.1.call-update
  9.2 0.7 convert_element_type.11
  9.9 0.8 copy.18
  10.8 0.7 pad_maximum_fusion.1
  11.5 10.2 %all-to-all-start.1 = ((f32[32,16,128]{2,1,0:T(8,128)}), f32[32,16,128]{2,1,0:T(8,128)S(1)}, u32[]{:S(2)}, u32[]{:S(2)}) async-start(f32[32,16,128]{2,1,0:T(8,128)} %pad_maximum_fusion.1), calls=%async_computation.1 | async-start | bytes 524288 | tf_op jit(solution)/shard_map/all_to_all | solution.py:144
  21.8 1.4 copy.15
  23.1 0.1 copy.16
  23.2 0.3 copy.17
  23.6 9.4 %all-to-all-done.1 = f32[32,16,128]{2,1,0:T(8,128)S(1)} async-done(((f32[32,16,128]{2,1,0:T(8,128)}), f32[32,16,128]{2,1,0:T(8,128)S(1)}, u32[]{:S(2)}, u32[]{:S(2)}) %all-to-all-start.1) | async-done | bytes 262176 | tf_op jit(solution)/shard_map/all_to_all | solution.py:144
  33.0 1.1 broadcast_in_dim.9
  34.1 3.6 %all-to-all-start = ((f32[8,64,512]{2,1,0:T(8,128)}), f32[8,64,512]{2,1,0:T(8,128)S(1)}, u32[]{:S(2)}, u32[]{:S(2)}) async-start(f32[8,64,512]{2,1,0:T(8,128)} %bitcast.4), calls=%async_computation | async-start | bytes 2097152 | tf_op jit(solution)/shard_map/all_to_all | solution.py:137
  37.7 27.4 %all-to-all-done.inv_ref = f32[8,64,512]{2,1,0:T(8,128)S(1)} async-done(((f32[8,64,512]{2,1,0:T(8,128)}), f32[8,64,512]{2,1,0:T(8,128)S(1)}, u32[]{:S(2)}, u32[]{:S(2)}) %all-to-all-start) | async-done | bytes 1048608 | tf_op jit(solution)/shard_map/all_to_all | solution.py:137
  65.1 9.0 %all-gather.3.cloned.1.call-done = f32[2048,1024]{1,0:T(8,128)} async-done(((f32[128,1024]{1,0:T(8,128)}), f32[2048,1024]{1,0:T(8,128)}) %all-gather.3.cloned.1.call-update) | async-done | bytes 8388624 | tf_op jit(solution)/shard_map/all_gather | solution.py:149
  74.0 0.0 copy-done.1
  74.0 0.0 copy-start
  74.1 3.4 %copy-done = f32[2048,1024]{1,0:T(8,128)S(1)} copy-done((f32[2048,1024]{1,0:T(8,128)S(1)}, f32[2048,1024]{1,0:T(8,128)}, u32[]{:S(2)}) %copy-start) | copy-done | bytes 8388632
  77.4 6.8 %solve.1 = (f32[1024,256]{1,0:T(8,128)}, f32[32,64,128]{2,1,0:T(8,128)S(1)}) custom-call(f32[16,128,1024]{2,1,0:T(8,128)S(1)} %bitcast.23, f32[1024,256]{1,0:T(8,128)S(1)} %copy-done.1), custom_call_target="tpu_custom_call" | custom-call | tf_op jit(solution)/shard_map/solve/pallas_call | solution.py:70
  84.2 38.1 %all_to_all.25.parts_ref = f32[32,64,128]{2,1,0:T(8,128)S(1)} all-to-all(f32[32,64,128]{2,1,0:T(8,128)S(1)} %get-tuple-element.13), channel_id=1, replica_groups=mesh['y'=8,'x'=4,'z'=8,'c'=2] {'y','x'}, dimensions={0} | all-to-all | bytes 2097152 | tf_op jit(solution)/shard_map/all_to_all | solution.py:153
  122.4 1.3 collect.1
  123.7 9.8 %all_to_all.26.column_ref = f32[4,128,128]{2,1,0:T(8,128)S(1)} all-to-all(f32[4,128,128]{2,1,0:T(8,128)S(1)} %collect.1), channel_id=1, replica_groups=mesh['y'=8,'x'=4,'z'=8,'c'=2] {'x'}, dimensions={0} | all-to-all | bytes 524288 | tf_op jit(solution)/shard_map/all_to_all | solution.py:154
  133.5 0.6 root.1
  134.1 12.9 %all_to_all.27 = f32[8,64,128]{2,1,0:T(8,128)S(1)} all-to-all(f32[8,64,128]{2,1,0:T(8,128)S(1)} %root.1), channel_id=1, replica_groups=mesh['y'=8,'x'=4,'z'=8,'c'=2] {'y'}, dimensions={0} | all-to-all | bytes 524288 | tf_op jit(solution)/shard_map/all_to_all | solution.py:155
  147.0 0.6 pad_maximum_fusion.2
  (9 shorter events, 0.1 us)
Async XLA Ops:
  7.2 66.9 %copy-start.1 = (f32[1024,256]{1,0:T(8,128)S(1)}, f32[1024,256]{1,0:T(8,128)}, u32[]{:S(2)}) copy-start(f32[1024,256]{1,0:T(8,128)} %rhs_ref.1) | copy-start | bytes 3145732
  7.2 66.9 %all-gather.3.cloned.1.call-start = ((), (), s32[]{:S(2)}) async-start(), calls=%async_computation.5 | async-start | bytes 8912896 | tf_op jit(solution)/shard_map/all_gather | solution.py:149
  11.5 21.5 %all-to-all-start.1 = ((f32[32,16,128]{2,1,0:T(8,128)}), f32[32,16,128]{2,1,0:T(8,128)S(1)}, u32[]{:S(2)}, u32[]{:S(2)}) async-start(f32[32,16,128]{2,1,0:T(8,128)} %pad_maximum_fusion.1), calls=%async_computation.1 | async-start | bytes 524288 | tf_op jit(solution)/shard_map/all_to_all | solution.py:144
  34.1 31.0 %all-to-all-start = ((f32[8,64,512]{2,1,0:T(8,128)}), f32[8,64,512]{2,1,0:T(8,128)S(1)}, u32[]{:S(2)}, u32[]{:S(2)}) async-start(f32[8,64,512]{2,1,0:T(8,128)} %bitcast.4), calls=%async_computation | async-start | bytes 2097152 | tf_op jit(solution)/shard_map/all_to_all | solution.py:137
  74.0 3.4 %copy-start = (f32[2048,1024]{1,0:T(8,128)S(1)}, f32[2048,1024]{1,0:T(8,128)}, u32[]{:S(2)}) copy-start(f32[2048,1024]{1,0:T(8,128)} %all-gather.3.cloned.1.call-done) | copy-start | bytes 25165828
Sparse Core Ops, SparseCore 0:
  10.1 63.9 all-gather.2

commit v4 on v3

--- a/solution.py
+++ b/solution.py
@@ -9,8 +9,9 @@
 BLK = 128
 NB = 16
 K = 8
-NY, NX, NZ, NC = 8, 4, 8, 2
-LEAF = ("y", "x")
+NA, NX, NZ, NC = 4, 4, 8, 2
+NEAR = 2 * NX
+LEAF = ("ya", "yb", "x")
 GRP = ("z", "c")
 SUB, LANE = 8, 128
 VMEM = pl.BlockSpec(memory_space=pltpu.VMEM)
@@ -57,11 +58,12 @@
         u = dot3(p_buf[i].reshape(part, width), s_hi[...], s_lo[...])
         for j in range(part // BLK):
             k = i * (part // BLK) + j
-            for y in range(NY):
-                for x in range(NX):
-                    r = BLK * j + SUB * (NX * (y // 2) + x)
-                    c = LANE * (y % 2)
-                    tiles_ref[NX * y + x, SUB * k : SUB * (k + 1), :] = u[r : r + SUB, c : c + LANE]
+            for a in range(NA):
+                for near in range(NEAR):
+                    r = BLK * j + SUB * (NX * a + near % NX)
+                    c = LANE * (near // NX)
+                    at = SUB * (NA * k + a)
+                    tiles_ref[near, at : at + SUB, :] = u[r : r + SUB, c : c + LANE]
 
 
 def solve(both, rhs, parts=2):
@@ -73,41 +75,42 @@
         out_specs=[VMEM, VMEM],
         out_shape=[
             jax.ShapeDtypeStruct((width, cols), jnp.float32),
-            jax.ShapeDtypeStruct((NY * NX, K * SUB, LANE), jnp.float32),
+            jax.ShapeDtypeStruct((NEAR, K * NA * SUB, LANE), jnp.float32),
         ],
         scratch_shapes=[pltpu.VMEM((parts, shards // parts, rows, width), jnp.float32)] * 2
         + [pltpu.VMEM((width, cols), jnp.bfloat16)] * 2
         + [pltpu.SemaphoreType.DMA((2 * parts,))],
-        compiler_params=pltpu.CompilerParams(vmem_limit_bytes=28 << 20),
+        compiler_params=pltpu.CompilerParams(vmem_limit_bytes=52 << 20),
         name="solve",
     )(both, rhs)
 
 
-def collect_kernel(index_ref, start_ref, parts_ref, out_ref, acc):
-    acc[...] = start_ref[...]
+def collect_kernel(index_ref, parts_ref, out_ref):
+    out_ref[...] = jnp.zeros_like(out_ref)
 
     def one(s, carry):
         at = [pl.multiple_of(index_ref[s, k] * SUB, SUB) for k in range(K)]
-        new = [acc[pl.ds(at[k], SUB), :] - parts_ref[s, SUB * k : SUB * (k + 1), :] for k in range(K)]
-        for k in range(K):
-            acc[pl.ds(at[k], SUB), :] = new[k]
+        for a in range(NA):
+            new = [
+                out_ref[a, pl.ds(at[k], SUB), :] + parts_ref[s, SUB * (NA * k + a) : SUB * (NA * k + a + 1), :]
+                for k in range(K)
+            ]
+            for k in range(K):
+                out_ref[a, pl.ds(at[k], SUB), :] = new[k]
         return carry
 
     lax.fori_loop(0, parts_ref.shape[0], one, 0)
-    for x in range(NX):
-        out_ref[x] = acc[...]
 
 
-def collect(index, start, parts):
+def collect(index, parts):
     return pl.pallas_call(
         collect_kernel,
-        in_specs=[SMEM, VMEM, VMEM],
+        in_specs=[SMEM, VMEM],
         out_specs=VMEM,
-        out_shape=jax.ShapeDtypeStruct((NX, NB * SUB, LANE), jnp.float32),
-        scratch_shapes=[pltpu.VMEM((NB * SUB, LANE), jnp.float32)],
+        out_shape=jax.ShapeDtypeStruct((NA, NB * SUB, LANE), jnp.float32),
         compiler_params=pltpu.CompilerParams(vmem_limit_bytes=12 << 20),
         name="collect",
-    )(index, start, parts)
+    )(index, parts)
 
 
 def root_kernel(inv_ref, column_ref, out_ref):
@@ -130,35 +133,38 @@
 
 def body(low_rhs, low_inverse, panels, row_blocks, root_rhs, root_inverse):
     own = root_rhs.shape[0]
-    y = lax.axis_index("y")
+    ya = lax.axis_index("ya")
 
-    some = BLK // 4
-    by_y = root_inverse.reshape(own, NB, 4, some).transpose(2, 0, 1, 3).reshape(4, 1, own, NB * some)
-    inv = lax.all_to_all(jnp.broadcast_to(by_y, (4, 2, own, NB * some)).reshape(NY, own, NB * some), "y", 0, 0)
+    some = BLK // NA
+    by_ya = root_inverse.reshape(own, NB, NA, some).transpose(2, 0, 1, 3).reshape(NA, 1, own, NB * some)
+    by_y = jnp.broadcast_to(by_ya, (NA, 2, own, NB * some)).reshape(2 * NA, own, NB * some)
+    inv = lax.all_to_all(by_y, ("ya", "yb"), 0, 0)
     rhs_tiles = root_rhs.reshape(2, NX, SUB, 2, LANE).transpose(0, 3, 1, 2, 4)
     rhs_tiles = jnp.broadcast_to(rhs_tiles[None], (2, 2, 2, NX, SUB, LANE))
     blocks = jnp.pad(row_blocks.astype(jnp.float32), ((0, SUB - 1), (0, LANE - K)))
     early = jnp.concatenate(
-        [rhs_tiles.reshape(NY * NX, SUB, LANE), jnp.broadcast_to(blocks[None], (NY * NX, SUB, LANE))], axis=1
+        [rhs_tiles.reshape(NA * NEAR, SUB, LANE), jnp.broadcast_to(blocks[None], (NA * NEAR, SUB, LANE))], axis=1
     )
     early = lax.all_to_all(early, LEAF, 0, 0)
-    index = early[:, SUB, :K].astype(jnp.int32)
-    start = lax.dynamic_index_in_dim(early[:, :SUB].reshape(NB, 2, SUB, LANE), y // 4, 1, keepdims=False)
+    index = lax.dynamic_slice_in_dim(early[:, SUB, :K].astype(jnp.int32), NEAR * ya, NEAR)
+    start = lax.dynamic_index_in_dim(early[:, :SUB].reshape(NB, 2, SUB, LANE), ya // 2, 1, keepdims=False)
     start = start.reshape(NB * SUB, LANE)
 
     both = lax.all_gather(jnp.concatenate([low_inverse, panels]), GRP, axis=0)
     both, inv, index, start = lax.optimization_barrier((both, inv, index, start))
 
     low_solution, tiles = solve(both, low_rhs)
-    parts = lax.all_to_all(tiles, LEAF, 0, 0)
-    column = lax.all_to_all(collect(index, start, parts), "x", 0, 0)
-    pieces = lax.all_to_all(root(inv, column), "y", 0, 0)
-    halves = jnp.sum(pieces.reshape(4, 2, own, LANE), axis=0)
+    parts = lax.all_to_all(tiles, ("yb", "x"), 0, 0)
+    sums = lax.all_to_all(collect(index, parts), "ya", 0, 0)
+    combined = start - jnp.sum(sums, axis=0)
+    column = lax.all_to_all(jnp.broadcast_to(combined[None], (NX, NB * SUB, LANE)), "x", 0, 0)
+    pieces = lax.all_to_all(root(inv, column), ("ya", "yb"), 0, 0)
+    halves = jnp.sum(pieces.reshape(NA, 2, own, LANE), axis=0)
     return (low_solution, jnp.concatenate([halves[0], halves[1]], axis=1))
 
 
 def solution(mesh):
-    fine = Mesh(mesh.devices.reshape(NY, NX, NZ, NC), LEAF + GRP)
+    fine = Mesh(mesh.devices.reshape(NA, 2, NX, NZ, NC), LEAF + GRP)
     placed = (
         P(LEAF, GRP),
         P(LEAF + GRP, None),

time: 155 us -> 151 us (0.974)
  local copies, waits for them, and re-layouts: 7.18 us -> 3.81 us
  blocking collectives: 60.8 us -> 58.6 us
    unnamed x5 -> x1, local copies, waits for them, and re-layouts: 4.76 us -> 1.37 us
    all_to_all x3 -> x4, blocking collectives: 60.8 us -> 58.6 us  [the longest x1 19.8 us: body(): parts = lax.all_to_all(tiles, ('yb', 'x'), 0, 0)]
    pallas_call x1, Pallas kernels: 6.78 us -> 8.37 us  [solve(): pl.pallas_call(solve_kernel, in_specs=[pl.BlockSpec(memory_space=pltpu.HB...]
where the time goes in v4:
time: 151 us; the launch traced here: 150 us
  blocking collectives  58.6 us (39%)
  waiting for transfers between devices  45.8 us (30%)
  between operations  14.2 us (9%)
  starting transfers between devices  13.8 us (9%)
  Pallas kernels  9.91 us (7%)
  other arithmetic  3.99 us (3%)
  local copies, waits for them, and re-layouts  3.81 us (3%)
    all_to_all x1, waiting for transfers between devices, body(): inv = lax.all_to_all(by_y, ('ya', 'yb'), 0, 0)  27.3 us
    all_to_all x1, blocking collectives, body(): parts = lax.all_to_all(tiles, ('yb', 'x'), 0, 0)  19.8 us
    all_to_all x1, blocking collectives, body(): sums = lax.all_to_all(collect(index, parts), 'ya', 0, 0)  16.4 us
    all_to_all x1, blocking collectives, body(): pieces = lax.all_to_all(root(inv, column), ('ya', 'yb'), 0, 0)  13.5 us
    all_to_all x1, starting transfers between devices, body(): early = lax.all_to_all(early, LEAF, 0, 0)  10.2 us
    all_to_all x1, waiting for transfers between devices, body(): early = lax.all_to_all(early, LEAF, 0, 0)  9.42 us
    all_gather x1, waiting for transfers between devices, body(): both = lax.all_gather(jnp.concatenate([low_inverse, panels]), GRP, axis=0)  9.03 us
    all_to_all x1, blocking collectives, body(): lax.all_to_all(jnp.broadcast_to(combined[None], (NX, NB * SUB, LANE)), 'x...  8.97 us
  transfers between devices with their start and end apart: 3, of which 3 were waited for; matrix products, arithmetic and copies ran while one was open for 3% of the time, Pallas kernels for 0%

profile of v4, /device:TPU:2, one launch (start us, length us, event | category | flops | bytes accessed | tf_op | source)
XLA Modules:
  0.0 150.2 jit_solution(10729941764085123830)
XLA Ops:
  7.2 0.0 all-gather.3.cloned.1.call-start
  7.2 1.9 %pad_maximum_fusion = f32[128,1024]{1,0:T(8,128)} fusion(f32[64,1024]{1,0:T(8,128)} %param.8, f32[64,1024]{1,0:T(8,128)} %param.7), kind=kLoop, calls=%fused_computation | loop fusion | flops 131072 | bytes 1048576 | tf_op jit(solution)/shard_map/concatenate | solution.py:153
  9.1 0.0 all-gather.3.cloned.1.call-update
  9.1 0.7 convert_element_type.9
  9.8 0.8 copy.18
  10.7 0.7 pad_maximum_fusion.1
  11.4 10.2 %all-to-all-start.1 = ((f32[32,16,128]{2,1,0:T(8,128)}), f32[32,16,128]{2,1,0:T(8,128)S(1)}, u32[]{:S(2)}, u32[]{:S(2)}) async-start(f32[32,16,128]{2,1,0:T(8,128)} %pad_maximum_fusion.1), calls=%async_computation.1 | async-start | bytes 524288 | tf_op jit(solution)/shard_map/all_to_all | solution.py:148
  21.7 1.4 copy.15
  23.1 0.1 copy.16
  23.1 0.3 copy.17
  23.5 9.4 %all-to-all-done.1 = f32[32,16,128]{2,1,0:T(8,128)S(1)} async-done(((f32[32,16,128]{2,1,0:T(8,128)}), f32[32,16,128]{2,1,0:T(8,128)S(1)}, u32[]{:S(2)}, u32[]{:S(2)}) %all-to-all-start.1) | async-done | bytes 262176 | tf_op jit(solution)/shard_map/all_to_all | solution.py:148
  32.9 1.1 broadcast_in_dim.11
  34.0 3.6 %all-to-all-start = ((f32[8,64,512]{2,1,0:T(8,128)}), f32[8,64,512]{2,1,0:T(8,128)S(1)}, u32[]{:S(2)}, u32[]{:S(2)}) async-start(f32[8,64,512]{2,1,0:T(8,128)} %bitcast.4), calls=%async_computation | async-start | bytes 2097152 | tf_op jit(solution)/shard_map/all_to_all | solution.py:141
  37.7 27.3 %all-to-all-done.inv_ref = f32[8,64,512]{2,1,0:T(8,128)S(1)} async-done(((f32[8,64,512]{2,1,0:T(8,128)}), f32[8,64,512]{2,1,0:T(8,128)S(1)}, u32[]{:S(2)}, u32[]{:S(2)}) %all-to-all-start) | async-done | bytes 1048608 | tf_op jit(solution)/shard_map/all_to_all | solution.py:141
  65.0 9.0 %all-gather.3.cloned.1.call-done = f32[2048,1024]{1,0:T(8,128)} async-done(((f32[128,1024]{1,0:T(8,128)}), f32[2048,1024]{1,0:T(8,128)}) %all-gather.3.cloned.1.call-update) | async-done | bytes 8388624 | tf_op jit(solution)/shard_map/all_gather | solution.py:153
  74.0 8.4 %solve.1 = (f32[1024,256]{1,0:T(8,128)}, f32[8,256,128]{2,1,0:T(8,128)S(1)}) custom-call(f32[16,128,1024]{2,1,0:T(8,128)} %bitcast.21, f32[1024,256]{1,0:T(8,128)} %rhs_ref.1), custom_call_target="tpu_custom_call" | custom-call | tf_op jit(solution)/shard_map/solve/pallas_call | solution.py:72
  82.4 19.8 %all_to_all.30.parts_ref = f32[8,256,128]{2,1,0:T(8,128)S(1)} all-to-all(f32[8,256,128]{2,1,0:T(8,128)S(1)} %get-tuple-element.13), channel_id=1, replica_groups=mesh['ya'=4,'yb'=2,'x'=4,'z'=8,'c'=2] {'yb','x'}, dimensions={0} | all-to-all | bytes 2097152 | tf_op jit(solution)/shard_map/all_to_all | solution.py:157
  102.2 1.0 collect.1
  103.1 16.4 %all_to_all.31 = f32[4,128,128]{2,1,0:T(8,128)S(1)} all-to-all(f32[4,128,128]{2,1,0:T(8,128)S(1)} %collect.1), channel_id=1, replica_groups=mesh['ya'=4,'yb'=2,'x'=4,'z'=8,'c'=2] {'ya'}, dimensions={0} | all-to-all | bytes 524288 | tf_op jit(solution)/shard_map/all_to_all | solution.py:158
  119.6 9.0 %all_to_all.32.column_ref = f32[4,128,128]{2,1,0:T(8,128)S(1)} all-to-all(f32[4,128,128]{2,1,0:T(8,128)S(1)} %broadcast_in_dim.14), channel_id=1, replica_groups=mesh['ya'=4,'yb'=2,'x'=4,'z'=8,'c'=2] {'x'}, dimensions={0} | all-to-all | bytes 524288 | tf_op jit(solution)/shard_map/all_to_all | solution.py:160
  128.6 0.6 root.1
  129.1 13.5 %all_to_all.33 = f32[8,64,128]{2,1,0:T(8,128)S(1)} all-to-all(f32[8,64,128]{2,1,0:T(8,128)S(1)} %root.1), channel_id=1, replica_groups=mesh['ya'=4,'yb'=2,'x'=4,'z'=8,'c'=2] {'ya','yb'}, dimensions={0} | all-to-all | bytes 524288 | tf_op jit(solution)/shard_map/all_to_all | solution.py:161
  142.7 0.6 pad_maximum_fusion.2
  (12 shorter events, 0.1 us)
Async XLA Ops:
  7.2 66.9 %all-gather.3.cloned.1.call-start = ((), (), s32[]{:S(2)}) async-start(), calls=%async_computation.6 | async-start | bytes 8912896 | tf_op jit(solution)/shard_map/all_gather | solution.py:153
  11.4 21.5 %all-to-all-start.1 = ((f32[32,16,128]{2,1,0:T(8,128)}), f32[32,16,128]{2,1,0:T(8,128)S(1)}, u32[]{:S(2)}, u32[]{:S(2)}) async-start(f32[32,16,128]{2,1,0:T(8,128)} %pad_maximum_fusion.1), calls=%async_computation.1 | async-start | bytes 524288 | tf_op jit(solution)/shard_map/all_to_all | solution.py:148
  34.0 31.0 %all-to-all-start = ((f32[8,64,512]{2,1,0:T(8,128)}), f32[8,64,512]{2,1,0:T(8,128)S(1)}, u32[]{:S(2)}, u32[]{:S(2)}) async-start(f32[8,64,512]{2,1,0:T(8,128)} %bitcast.4), calls=%async_computation | async-start | bytes 2097152 | tf_op jit(solution)/shard_map/all_to_all | solution.py:141
Sparse Core Ops, SparseCore 0:
  10.1 63.9 all-gather.2

commit v5 on v4

--- a/solution.py
+++ b/solution.py
@@ -29,60 +29,89 @@
     return d(hi, b_hi) + (d(hi, b_lo) + d(lo, b_hi))
 
 
-def solve_kernel(both_ref, rhs_ref, low_ref, tiles_ref, l_buf, p_buf, s_hi, s_lo, sems):
-    parts, shards, rows, width = l_buf.shape
+def solve_kernel(both_ref, r_hi, r_lo, low_ref, tiles_ref, pieces, hi, lo, s_hi, s_lo, low, sems, low_sem):
+    count, shards, rows, width = pieces.shape
+    parts = count // 2
     part = shards * rows
+    deep = [min((i + 1) * part, width) for i in range(count)]
 
     def read(i):
-        here = pl.ds(shards * (i % parts), shards)
-        if i < parts:
-            deep = pl.ds(0, (i + 1) * part)
-            src, dst = both_ref.at[here, pl.ds(0, rows), deep], l_buf.at[i, :, :, deep]
-        else:
-            src, dst = both_ref.at[here, pl.ds(rows, rows), :], p_buf.at[i - parts]
-        return pltpu.make_async_copy(src, dst, sems.at[i])
-
-    reads = [read(i) for i in range(2 * parts)]
+        here, which = pl.ds(shards * (i % parts), shards), pl.ds(rows * (i // parts), rows)
+        depth = pl.ds(0, deep[i])
+        return pltpu.make_async_copy(both_ref.at[here, which, depth], pieces.at[i, :, :, depth], sems.at[i])
+
+    reads = [read(i) for i in range(count)]
     for copy in reads:
         copy.start()
-    r_hi, r_lo = split(rhs_ref[...])
-    for i in range(parts):
-        reads[i].wait()
-        deep = (i + 1) * part
-        s = dot3(l_buf[i].reshape(part, width)[:, :deep], r_hi[:deep], r_lo[:deep])
-        here = pl.ds(i * part, part)
-        low_ref[here, :] = s
-        s_hi[here, :], s_lo[here, :] = split(s)
-    for i in range(parts):
-        reads[parts + i].wait()
-        u = dot3(p_buf[i].reshape(part, width), s_hi[...], s_lo[...])
-        for j in range(part // BLK):
-            k = i * (part // BLK) + j
-            for a in range(NA):
-                for near in range(NEAR):
-                    r = BLK * j + SUB * (NX * a + near % NX)
-                    c = LANE * (near // NX)
-                    at = SUB * (NA * k + a)
-                    tiles_ref[near, at : at + SUB, :] = u[r : r + SUB, c : c + LANE]
-
-
-def solve(both, rhs, parts=2):
+    d = lambda u, v: jnp.dot(u, v, preferred_element_type=jnp.float32)
+
+    def cut(i):
+        hi[i, :, : deep[i]], lo[i, :, : deep[i]] = split(pieces[i].reshape(part, width)[:, : deep[i]])
+
+    reads[0].wait()
+    cut(0)
+    for i in range(count):
+        if i + 1 < count:
+            reads[i + 1].wait()
+            cut(i + 1)
+        n = deep[i]
+        a_hi, a_lo = hi[i, :, :n], lo[i, :, :n]
+        b_hi, b_lo = (r_hi[:n], r_lo[:n]) if i < parts else (s_hi[...], s_lo[...])
+        out = d(a_hi, b_hi) + (d(a_hi, b_lo) + d(a_lo, b_hi))
+        if i < parts:
+            here = pl.ds(i * part, part)
+            low[here, :] = out
+            s_hi[here, :], s_lo[here, :] = split(out)
+        if i == parts - 1:
+            done = pltpu.make_async_copy(low, low_ref, low_sem)
+            done.start()
+        if i >= parts:
+            for j in range(part // BLK):
+                k = (i - parts) * (part // BLK) + j
+                for a in range(NA):
+                    for near in range(NEAR):
+                        r = BLK * j + SUB * (NX * a + near % NX)
+                        c = LANE * (near // NX)
+                        at = SUB * (NA * k + a)
+                        tiles_ref[near, at : at + SUB, :] = out[r : r + SUB, c : c + LANE]
+    done.wait()
+
+
+def solve(both, rhs_hi, rhs_lo, parts=2):
     shards, rows2, width = both.shape
-    rows, cols = rows2 // 2, rhs.shape[1]
+    rows, cols = rows2 // 2, rhs_hi.shape[1]
+    part = width // parts
     return pl.pallas_call(
         solve_kernel,
-        in_specs=[pl.BlockSpec(memory_space=pltpu.HBM), VMEM],
-        out_specs=[VMEM, VMEM],
+        in_specs=[pl.BlockSpec(memory_space=pltpu.HBM), VMEM, VMEM],
+        out_specs=[pl.BlockSpec(memory_space=pltpu.HBM), VMEM],
         out_shape=[
             jax.ShapeDtypeStruct((width, cols), jnp.float32),
             jax.ShapeDtypeStruct((NEAR, K * NA * SUB, LANE), jnp.float32),
         ],
-        scratch_shapes=[pltpu.VMEM((parts, shards // parts, rows, width), jnp.float32)] * 2
+        scratch_shapes=[pltpu.VMEM((2 * parts, shards // parts, rows, width), jnp.float32)]
+        + [pltpu.VMEM((2 * parts, part, width), jnp.bfloat16)] * 2
         + [pltpu.VMEM((width, cols), jnp.bfloat16)] * 2
-        + [pltpu.SemaphoreType.DMA((2 * parts,))],
+        + [pltpu.VMEM((width, cols), jnp.float32)]
+        + [pltpu.SemaphoreType.DMA((2 * parts,)), pltpu.SemaphoreType.DMA(())],
         compiler_params=pltpu.CompilerParams(vmem_limit_bytes=52 << 20),
         name="solve",
-    )(both, rhs)
+    )(both, rhs_hi, rhs_lo)
+
+
+def split_kernel(a_ref, hi_ref, lo_ref):
+    hi_ref[...], lo_ref[...] = split(a_ref[...])
+
+
+def split_ahead(a):
+    return pl.pallas_call(
+        split_kernel,
+        in_specs=[VMEM],
+        out_specs=[VMEM, VMEM],
+        out_shape=[jax.ShapeDtypeStruct(a.shape, jnp.bfloat16)] * 2,
+        compiler_params=pltpu.CompilerParams(vmem_limit_bytes=12 << 20),
+        name="split_ahead",
+    )(a)
 
 
 def collect_kernel(index_ref, parts_ref, out_ref):
@@ -151,9 +180,10 @@
     start = start.reshape(NB * SUB, LANE)
 
     both = lax.all_gather(jnp.concatenate([low_inverse, panels]), GRP, axis=0)
-    both, inv, index, start = lax.optimization_barrier((both, inv, index, start))
-
-    low_solution, tiles = solve(both, low_rhs)
+    rhs_hi, rhs_lo = split_ahead(low_rhs)
+    both, inv, index, start, rhs_hi, rhs_lo = lax.optimization_barrier((both, inv, index, start, rhs_hi, rhs_lo))
+
+    low_solution, tiles = solve(both, rhs_hi, rhs_lo)
     parts = lax.all_to_all(tiles, ("yb", "x"), 0, 0)
     sums = lax.all_to_all(collect(index, parts), "ya", 0, 0)
     combined = start - jnp.sum(sums, axis=0)

time: 151 us -> 150 us (level)
  no operation moved by 1% of the time
where the time goes in v5:
time: 150 us
  blocking collectives  58.8 us (39%)
  waiting for transfers between devices  45.6 us (30%)
  between operations  14.2 us (9%)
  starting transfers between devices  13.8 us (9%)
  Pallas kernels  9.46 us (6%)
  other arithmetic  4.07 us (3%)
  local copies, waits for them, and re-layouts  3.81 us (3%)
    all_to_all x1, waiting for transfers between devices, body(): inv = lax.all_to_all(by_y, ('ya', 'yb'), 0, 0)  27.2 us
    all_to_all x1, blocking collectives, body(): parts = lax.all_to_all(tiles, ('yb', 'x'), 0, 0)  20 us
    all_to_all x1, blocking collectives, body(): sums = lax.all_to_all(collect(index, parts), 'ya', 0, 0)  16.4 us
    all_to_all x1, blocking collectives, body(): pieces = lax.all_to_all(root(inv, column), ('ya', 'yb'), 0, 0)  13.5 us
    all_to_all x1, starting transfers between devices, body(): early = lax.all_to_all(early, LEAF, 0, 0)  10.2 us
    all_to_all x1, waiting for transfers between devices, body(): early = lax.all_to_all(early, LEAF, 0, 0)  9.42 us
    all_to_all x1, blocking collectives, body(): lax.all_to_all(jnp.broadcast_to(combined[None], (NX, NB * SUB, LANE)), 'x...  8.97 us
    all_gather x1, waiting for transfers between devices, body(): both = lax.all_gather(jnp.concatenate([low_inverse, panels]), GRP, axis=0)  8.95 us
  transfers between devices with their start and end apart: 3, of which 3 were waited for; matrix products, arithmetic and copies ran while one was open for 3% of the time, Pallas kernels for 0%

profile of v5, /device:TPU:2, one launch (start us, length us, event | category | flops | bytes accessed | tf_op | source)
XLA Modules:
  0.0 149.8 jit_solution(15146632444631461941)
XLA Ops:
  7.2 0.0 copy-start
  7.2 0.0 all-gather.3.cloned.1.call-start
  7.2 2.0 %pad_maximum_fusion = f32[128,1024]{1,0:T(8,128)} fusion(f32[64,1024]{1,0:T(8,128)} %param.8, f32[64,1024]{1,0:T(8,128)} %param.7), kind=kLoop, calls=%fused_computation | loop fusion | flops 131072 | bytes 1048576 | tf_op jit(solution)/shard_map/concatenate | solution.py:182
  9.2 0.0 all-gather.3.cloned.1.call-update
  9.2 0.7 convert_element_type.9
  9.9 0.8 copy.18
  10.8 0.7 pad_maximum_fusion.1
  11.5 10.2 %all-to-all-start.1 = ((f32[32,16,128]{2,1,0:T(8,128)}), f32[32,16,128]{2,1,0:T(8,128)S(1)}, u32[]{:S(2)}, u32[]{:S(2)}) async-start(f32[32,16,128]{2,1,0:T(8,128)} %pad_maximum_fusion.1), calls=%async_computation.1 | async-start | bytes 524288 | tf_op jit(solution)/shard_map/all_to_all | solution.py:177
  21.8 1.4 copy.15
  23.1 0.1 copy.16
  23.2 0.3 copy.17
  23.6 9.4 %all-to-all-done.1 = f32[32,16,128]{2,1,0:T(8,128)S(1)} async-done(((f32[32,16,128]{2,1,0:T(8,128)}), f32[32,16,128]{2,1,0:T(8,128)S(1)}, u32[]{:S(2)}, u32[]{:S(2)}) %all-to-all-start.1) | async-done | bytes 262176 | tf_op jit(solution)/shard_map/all_to_all | solution.py:177
  33.0 1.1 broadcast_in_dim.11
  34.1 3.6 %all-to-all-start = ((f32[8,64,512]{2,1,0:T(8,128)}), f32[8,64,512]{2,1,0:T(8,128)S(1)}, u32[]{:S(2)}, u32[]{:S(2)}) async-start(f32[8,64,512]{2,1,0:T(8,128)} %bitcast.4), calls=%async_computation | async-start | bytes 2097152 | tf_op jit(solution)/shard_map/all_to_all | solution.py:170
  37.7 0.0 copy-done
  37.7 0.1 split_ahead.1
  37.9 27.2 %all-to-all-done.inv_ref = f32[8,64,512]{2,1,0:T(8,128)S(1)} async-done(((f32[8,64,512]{2,1,0:T(8,128)}), f32[8,64,512]{2,1,0:T(8,128)S(1)}, u32[]{:S(2)}, u32[]{:S(2)}) %all-to-all-start) | async-done | bytes 1048608 | tf_op jit(solution)/shard_map/all_to_all | solution.py:170
  65.1 8.9 %all-gather.3.cloned.1.call-done = f32[2048,1024]{1,0:T(8,128)} async-done(((f32[128,1024]{1,0:T(8,128)}), f32[2048,1024]{1,0:T(8,128)}) %all-gather.3.cloned.1.call-update) | async-done | bytes 8388624 | tf_op jit(solution)/shard_map/all_gather | solution.py:182
  74.0 7.8 %solve.1 = (f32[1024,256]{1,0:T(8,128)}, f32[8,256,128]{2,1,0:T(8,128)}) custom-call(f32[16,128,1024]{2,1,0:T(8,128)} %bitcast.21, bf16[1024,256]{1,0:T(8,128)(2,1)S(1)} %get-tuple-element.15.r_hi, bf16[1024,256]{1,0:T(8,128)(2,1)S(1)} %get-tuple-element.16.r_lo), custom_call_target="tpu_custom_call" | custom-call | tf_op jit(solution)/shard_map/solve/pallas_call | solution.py:84
  81.8 20.0 %all_to_all.30.parts_ref = f32[8,256,128]{2,1,0:T(8,128)S(1)} all-to-all(f32[8,256,128]{2,1,0:T(8,128)} %get-tuple-element.21), channel_id=1, replica_groups=mesh['ya'=4,'yb'=2,'x'=4,'z'=8,'c'=2] {'yb','x'}, dimensions={0} | all-to-all | bytes 2097152 | tf_op jit(solution)/shard_map/all_to_all | solution.py:187
  101.8 1.0 collect.1
  102.8 16.4 %all_to_all.31 = f32[4,128,128]{2,1,0:T(8,128)S(1)} all-to-all(f32[4,128,128]{2,1,0:T(8,128)S(1)} %collect.1), channel_id=1, replica_groups=mesh['ya'=4,'yb'=2,'x'=4,'z'=8,'c'=2] {'ya'}, dimensions={0} | all-to-all | bytes 524288 | tf_op jit(solution)/shard_map/all_to_all | solution.py:188
  119.2 9.0 %all_to_all.32.column_ref = f32[4,128,128]{2,1,0:T(8,128)S(1)} all-to-all(f32[4,128,128]{2,1,0:T(8,128)S(1)} %broadcast_in_dim.14), channel_id=1, replica_groups=mesh['ya'=4,'yb'=2,'x'=4,'z'=8,'c'=2] {'x'}, dimensions={0} | all-to-all | bytes 524288 | tf_op jit(solution)/shard_map/all_to_all | solution.py:190
  128.2 0.6 root.1
  128.8 13.5 %all_to_all.33 = f32[8,64,128]{2,1,0:T(8,128)S(1)} all-to-all(f32[8,64,128]{2,1,0:T(8,128)S(1)} %root.1), channel_id=1, replica_groups=mesh['ya'=4,'yb'=2,'x'=4,'z'=8,'c'=2] {'ya','yb'}, dimensions={0} | all-to-all | bytes 524288 | tf_op jit(solution)/shard_map/all_to_all | solution.py:191
  142.3 0.6 pad_maximum_fusion.2
  (12 shorter events, 0.1 us)
Async XLA Ops:
  7.2 30.5 %copy-start = (f32[1024,256]{1,0:T(8,128)S(1)}, f32[1024,256]{1,0:T(8,128)}, u32[]{:S(2)}) copy-start(f32[1024,256]{1,0:T(8,128)} %a_ref.1) | copy-start | bytes 3145732
  7.2 66.9 %all-gather.3.cloned.1.call-start = ((), (), s32[]{:S(2)}) async-start(), calls=%async_computation.6 | async-start | bytes 8912896 | tf_op jit(solution)/shard_map/all_gather | solution.py:182
  11.5 21.5 %all-to-all-start.1 = ((f32[32,16,128]{2,1,0:T(8,128)}), f32[32,16,128]{2,1,0:T(8,128)S(1)}, u32[]{:S(2)}, u32[]{:S(2)}) async-start(f32[32,16,128]{2,1,0:T(8,128)} %pad_maximum_fusion.1), calls=%async_computation.1 | async-start | bytes 524288 | tf_op jit(solution)/shard_map/all_to_all | solution.py:177
  34.1 31.0 %all-to-all-start = ((f32[8,64,512]{2,1,0:T(8,128)}), f32[8,64,512]{2,1,0:T(8,128)S(1)}, u32[]{:S(2)}, u32[]{:S(2)}) async-start(f32[8,64,512]{2,1,0:T(8,128)} %bitcast.4), calls=%async_computation | async-start | bytes 2097152 | tf_op jit(solution)/shard_map/all_to_all | solution.py:170
Sparse Core Ops, SparseCore 0:
  10.1 63.9 all-gather.2

commit v6 on v5

--- a/solution.py
+++ b/solution.py
@@ -36,9 +36,9 @@
     deep = [min((i + 1) * part, width) for i in range(count)]
 
     def read(i):
-        here, which = pl.ds(shards * (i % parts), shards), pl.ds(rows * (i // parts), rows)
-        depth = pl.ds(0, deep[i])
-        return pltpu.make_async_copy(both_ref.at[here, which, depth], pieces.at[i, :, :, depth], sems.at[i])
+        here = pl.ds(shards * (i % parts), shards)
+        src = both_ref.at[here, :, pl.ds(width * (i // parts), deep[i])]
+        return pltpu.make_async_copy(src, pieces.at[i, :, :, pl.ds(0, deep[i])], sems.at[i])
 
     reads = [read(i) for i in range(count)]
     for copy in reads:
@@ -78,8 +78,8 @@
 
 
 def solve(both, rhs_hi, rhs_lo, parts=2):
-    shards, rows2, width = both.shape
-    rows, cols = rows2 // 2, rhs_hi.shape[1]
+    shards, rows, _ = both.shape
+    width, cols = rhs_hi.shape
     part = width // parts
     return pl.pallas_call(
         solve_kernel,
@@ -179,7 +179,7 @@
     start = lax.dynamic_index_in_dim(early[:, :SUB].reshape(NB, 2, SUB, LANE), ya // 2, 1, keepdims=False)
     start = start.reshape(NB * SUB, LANE)
 
-    both = lax.all_gather(jnp.concatenate([low_inverse, panels]), GRP, axis=0)
+    both = lax.all_gather(jnp.concatenate([low_inverse, panels], axis=1), GRP, axis=0)
     rhs_hi, rhs_lo = split_ahead(low_rhs)
     both, inv, index, start, rhs_hi, rhs_lo = lax.optimization_barrier((both, inv, index, start, rhs_hi, rhs_lo))
 

time: 150 us -> 150 us (level)
  no operation moved by 1% of the time
where the time goes in v6:
time: 150 us
  blocking collectives  58.8 us (39%)
  waiting for transfers between devices  45.6 us (30%)
  between operations  14.2 us (9%)
  starting transfers between devices  13.8 us (9%)
  Pallas kernels  9.46 us (6%)
  other arithmetic  4.06 us (3%)
  local copies, waits for them, and re-layouts  3.81 us (3%)
    all_to_all x1, waiting for transfers between devices, body(): inv = lax.all_to_all(by_y, ('ya', 'yb'), 0, 0)  27.2 us
    all_to_all x1, blocking collectives, body(): parts = lax.all_to_all(tiles, ('yb', 'x'), 0, 0)  20 us
    all_to_all x1, blocking collectives, body(): sums = lax.all_to_all(collect(index, parts), 'ya', 0, 0)  16.4 us
    all_to_all x1, blocking collectives, body(): pieces = lax.all_to_all(root(inv, column), ('ya', 'yb'), 0, 0)  13.5 us
    all_to_all x1, starting transfers between devices, body(): early = lax.all_to_all(early, LEAF, 0, 0)  10.2 us
    all_to_all x1, waiting for transfers between devices, body(): early = lax.all_to_all(early, LEAF, 0, 0)  9.42 us
    all_to_all x1, blocking collectives, body(): lax.all_to_all(jnp.broadcast_to(combined[None], (NX, NB * SUB, LANE)), 'x...  8.97 us
    all_gather x1, waiting for transfers between devices, body(): lax.all_gather(jnp.concatenate([low_inverse, panels], axis=1), GRP, axis=0)  8.96 us
  transfers between devices with their start and end apart: 3, of which 3 were waited for; matrix products, arithmetic and copies ran while one was open for 3% of the time, Pallas kernels for 0%

profile of v6, /device:TPU:2, one launch (start us, length us, event | category | flops | bytes accessed | tf_op | source)
XLA Modules:
  0.0 149.8 jit_solution(11881761059627549660)
XLA Ops:
  7.2 0.0 copy-start
  7.2 0.0 all-gather.3.cloned.1.call-start
  7.2 2.0 %pad_maximum_fusion = f32[64,2048]{1,0:T(8,128)} fusion(f32[64,1024]{1,0:T(8,128)} %param.8, f32[64,1024]{1,0:T(8,128)} %param.7), kind=kLoop, calls=%fused_computation | loop fusion | flops 131072 | bytes 1048576 | tf_op jit(solution)/shard_map/concatenate | solution.py:182
  9.2 0.0 all-gather.3.cloned.1.call-update
  9.2 0.7 convert_element_type.9
  9.9 0.8 copy.18
  10.8 0.7 pad_maximum_fusion.1
  11.5 10.2 %all-to-all-start.1 = ((f32[32,16,128]{2,1,0:T(8,128)}), f32[32,16,128]{2,1,0:T(8,128)S(1)}, u32[]{:S(2)}, u32[]{:S(2)}) async-start(f32[32,16,128]{2,1,0:T(8,128)} %pad_maximum_fusion.1), calls=%async_computation.1 | async-start | bytes 524288 | tf_op jit(solution)/shard_map/all_to_all | solution.py:177
  21.8 1.4 copy.15
  23.1 0.1 copy.16
  23.2 0.3 copy.17
  23.5 9.4 %all-to-all-done.1 = f32[32,16,128]{2,1,0:T(8,128)S(1)} async-done(((f32[32,16,128]{2,1,0:T(8,128)}), f32[32,16,128]{2,1,0:T(8,128)S(1)}, u32[]{:S(2)}, u32[]{:S(2)}) %all-to-all-start.1) | async-done | bytes 262176 | tf_op jit(solution)/shard_map/all_to_all | solution.py:177
  33.0 1.1 broadcast_in_dim.11
  34.1 3.6 %all-to-all-start = ((f32[8,64,512]{2,1,0:T(8,128)}), f32[8,64,512]{2,1,0:T(8,128)S(1)}, u32[]{:S(2)}, u32[]{:S(2)}) async-start(f32[8,64,512]{2,1,0:T(8,128)} %bitcast.4), calls=%async_computation | async-start | bytes 2097152 | tf_op jit(solution)/shard_map/all_to_all | solution.py:170
  37.7 0.0 copy-done
  37.7 0.1 split_ahead.1
  37.9 27.2 %all-to-all-done.inv_ref = f32[8,64,512]{2,1,0:T(8,128)S(1)} async-done(((f32[8,64,512]{2,1,0:T(8,128)}), f32[8,64,512]{2,1,0:T(8,128)S(1)}, u32[]{:S(2)}, u32[]{:S(2)}) %all-to-all-start) | async-done | bytes 1048608 | tf_op jit(solution)/shard_map/all_to_all | solution.py:170
  65.1 9.0 %all-gather.3.cloned.1.call-done = f32[1024,2048]{1,0:T(8,128)} async-done(((f32[64,2048]{1,0:T(8,128)}), f32[1024,2048]{1,0:T(8,128)}) %all-gather.3.cloned.1.call-update) | async-done | bytes 8388624 | tf_op jit(solution)/shard_map/all_gather | solution.py:182
  74.0 7.8 %solve.1 = (f32[1024,256]{1,0:T(8,128)}, f32[8,256,128]{2,1,0:T(8,128)}) custom-call(f32[16,64,2048]{2,1,0:T(8,128)} %bitcast.21, bf16[1024,256]{1,0:T(8,128)(2,1)S(1)} %get-tuple-element.15.r_hi, bf16[1024,256]{1,0:T(8,128)(2,1)S(1)} %get-tuple-element.16.r_lo), custom_call_target="tpu_custom_call" | custom-call | tf_op jit(solution)/shard_map/solve/pallas_call | solution.py:84
  81.8 20.0 %all_to_all.30.parts_ref = f32[8,256,128]{2,1,0:T(8,128)S(1)} all-to-all(f32[8,256,128]{2,1,0:T(8,128)} %get-tuple-element.21), channel_id=1, replica_groups=mesh['ya'=4,'yb'=2,'x'=4,'z'=8,'c'=2] {'yb','x'}, dimensions={0} | all-to-all | bytes 2097152 | tf_op jit(solution)/shard_map/all_to_all | solution.py:187
  101.8 1.0 collect.1
  102.8 16.4 %all_to_all.31 = f32[4,128,128]{2,1,0:T(8,128)S(1)} all-to-all(f32[4,128,128]{2,1,0:T(8,128)S(1)} %collect.1), channel_id=1, replica_groups=mesh['ya'=4,'yb'=2,'x'=4,'z'=8,'c'=2] {'ya'}, dimensions={0} | all-to-all | bytes 524288 | tf_op jit(solution)/shard_map/all_to_all | solution.py:188
  119.2 9.0 %all_to_all.32.column_ref = f32[4,128,128]{2,1,0:T(8,128)S(1)} all-to-all(f32[4,128,128]{2,1,0:T(8,128)S(1)} %broadcast_in_dim.14), channel_id=1, replica_groups=mesh['ya'=4,'yb'=2,'x'=4,'z'=8,'c'=2] {'x'}, dimensions={0} | all-to-all | bytes 524288 | tf_op jit(solution)/shard_map/all_to_all | solution.py:190
  128.2 0.6 root.1
  128.8 13.5 %all_to_all.33 = f32[8,64,128]{2,1,0:T(8,128)S(1)} all-to-all(f32[8,64,128]{2,1,0:T(8,128)S(1)} %root.1), channel_id=1, replica_groups=mesh['ya'=4,'yb'=2,'x'=4,'z'=8,'c'=2] {'ya','yb'}, dimensions={0} | all-to-all | bytes 524288 | tf_op jit(solution)/shard_map/all_to_all | solution.py:191
  142.3 0.6 pad_maximum_fusion.2
  (12 shorter events, 0.1 us)
Async XLA Ops:
  7.2 30.5 %copy-start = (f32[1024,256]{1,0:T(8,128)S(1)}, f32[1024,256]{1,0:T(8,128)}, u32[]{:S(2)}) copy-start(f32[1024,256]{1,0:T(8,128)} %a_ref.1) | copy-start | bytes 3145732
  7.2 66.9 %all-gather.3.cloned.1.call-start = ((), (), s32[]{:S(2)}) async-start(), calls=%async_computation.6 | async-start | bytes 8912896 | tf_op jit(solution)/shard_map/all_gather | solution.py:182
  11.5 21.5 %all-to-all-start.1 = ((f32[32,16,128]{2,1,0:T(8,128)}), f32[32,16,128]{2,1,0:T(8,128)S(1)}, u32[]{:S(2)}, u32[]{:S(2)}) async-start(f32[32,16,128]{2,1,0:T(8,128)} %pad_maximum_fusion.1), calls=%async_computation.1 | async-start | bytes 524288 | tf_op jit(solution)/shard_map/all_to_all | solution.py:177
  34.1 31.0 %all-to-all-start = ((f32[8,64,512]{2,1,0:T(8,128)}), f32[8,64,512]{2,1,0:T(8,128)S(1)}, u32[]{:S(2)}, u32[]{:S(2)}) async-start(f32[8,64,512]{2,1,0:T(8,128)} %bitcast.4), calls=%async_computation | async-start | bytes 2097152 | tf_op jit(solution)/shard_map/all_to_all | solution.py:170
Sparse Core Ops, SparseCore 0:
  10.1 63.9 all-gather.2

commit v7 on v6

--- a/solution.py
+++ b/solution.py
@@ -142,22 +142,24 @@
     )(index, parts)
 
 
-def root_kernel(inv_ref, column_ref, out_ref):
+def root_kernel(inv_hi, inv_lo, column_ref, out_ref):
     tiles = [column_ref[x, SUB * b : SUB * (b + 1), :] for b in range(NB) for x in range(NX)]
     hi, lo = split(jnp.concatenate(tiles))
-    out = dot3(inv_ref[...].reshape(-1, inv_ref.shape[2]), hi, lo)
+    a_hi, a_lo = [ref[...].reshape(-1, ref.shape[2]) for ref in (inv_hi, inv_lo)]
+    d = lambda u, v: jnp.dot(u, v, preferred_element_type=jnp.float32)
+    out = d(a_hi, hi) + (d(a_hi, lo) + d(a_lo, hi))
     out_ref[...] = out.reshape(out_ref.shape)
 
 
-def root(inv, column):
+def root(inv_hi, inv_lo, column):
     return pl.pallas_call(
         root_kernel,
-        in_specs=[VMEM, VMEM],
+        in_specs=[VMEM, VMEM, VMEM],
         out_specs=VMEM,
-        out_shape=jax.ShapeDtypeStruct((inv.shape[0], inv.shape[1], LANE), jnp.float32),
+        out_shape=jax.ShapeDtypeStruct((inv_hi.shape[0], inv_hi.shape[1], LANE), jnp.float32),
         compiler_params=pltpu.CompilerParams(vmem_limit_bytes=12 << 20),
         name="root",
-    )(inv, column)
+    )(inv_hi, inv_lo, column)
 
 
 def body(low_rhs, low_inverse, panels, row_blocks, root_rhs, root_inverse):
@@ -181,6 +183,7 @@
 
     both = lax.all_gather(jnp.concatenate([low_inverse, panels], axis=1), GRP, axis=0)
     rhs_hi, rhs_lo = split_ahead(low_rhs)
+    inv = split_ahead(inv)
     both, inv, index, start, rhs_hi, rhs_lo = lax.optimization_barrier((both, inv, index, start, rhs_hi, rhs_lo))
 
     low_solution, tiles = solve(both, rhs_hi, rhs_lo)
@@ -188,7 +191,7 @@
     sums = lax.all_to_all(collect(index, parts), "ya", 0, 0)
     combined = start - jnp.sum(sums, axis=0)
     column = lax.all_to_all(jnp.broadcast_to(combined[None], (NX, NB * SUB, LANE)), "x", 0, 0)
-    pieces = lax.all_to_all(root(inv, column), ("ya", "yb"), 0, 0)
+    pieces = lax.all_to_all(root(*inv, column), ("ya", "yb"), 0, 0)
     halves = jnp.sum(pieces.reshape(NA, 2, own, LANE), axis=0)
     return (low_solution, jnp.concatenate([halves[0], halves[1]], axis=1))
 

time: 150 us -> 150 us (level)
  no operation moved by 1% of the time
where the time goes in v7:
time: 150 us
  blocking collectives  58.8 us (39%)
  waiting for transfers between devices  45.4 us (30%)
  between operations  14.2 us (9%)
  starting transfers between devices  13.8 us (9%)
  Pallas kernels  9.6 us (6%)
  other arithmetic  4.05 us (3%)
  local copies, waits for them, and re-layouts  3.81 us (3%)
    all_to_all x1, waiting for transfers between devices, body(): inv = lax.all_to_all(by_y, ('ya', 'yb'), 0, 0)  27.2 us
    all_to_all x1, blocking collectives, body(): parts = lax.all_to_all(tiles, ('yb', 'x'), 0, 0)  20 us
    all_to_all x1, blocking collectives, body(): sums = lax.all_to_all(collect(index, parts), 'ya', 0, 0)  16.4 us
    all_to_all x1, blocking collectives, body(): pieces = lax.all_to_all(root(*inv, column), ('ya', 'yb'), 0, 0)  13.5 us
    all_to_all x1, starting transfers between devices, body(): early = lax.all_to_all(early, LEAF, 0, 0)  10.2 us
    all_to_all x1, waiting for transfers between devices, body(): early = lax.all_to_all(early, LEAF, 0, 0)  9.42 us
    all_to_all x1, blocking collectives, body(): lax.all_to_all(jnp.broadcast_to(combined[None], (NX, NB * SUB, LANE)), 'x...  8.97 us
    all_gather x1, waiting for transfers between devices, body(): lax.all_gather(jnp.concatenate([low_inverse, panels], axis=1), GRP, axis=0)  8.82 us
  transfers between devices with their start and end apart: 3, of which 3 were waited for; matrix products, arithmetic and copies ran while one was open for 3% of the time, Pallas kernels for 0%

profile of v7, /device:TPU:2, one launch (start us, length us, event | category | flops | bytes accessed | tf_op | source)
XLA Modules:
  0.0 149.8 jit_solution(7517283964045597705)
XLA Ops:
  7.2 0.0 copy-start
  7.2 0.0 all-gather.3.cloned.1.call-start
  7.2 2.0 %pad_maximum_fusion = f32[64,2048]{1,0:T(8,128)} fusion(f32[64,1024]{1,0:T(8,128)} %param.8, f32[64,1024]{1,0:T(8,128)} %param.7), kind=kLoop, calls=%fused_computation | loop fusion | flops 131072 | bytes 1048576 | tf_op jit(solution)/shard_map/concatenate | solution.py:184
  9.2 0.0 all-gather.3.cloned.1.call-update
  9.2 0.7 convert_element_type.9
  9.9 0.8 copy.18
  10.8 0.7 pad_maximum_fusion.1
  11.5 10.2 %all-to-all-start.1 = ((f32[32,16,128]{2,1,0:T(8,128)}), f32[32,16,128]{2,1,0:T(8,128)S(1)}, u32[]{:S(2)}, u32[]{:S(2)}) async-start(f32[32,16,128]{2,1,0:T(8,128)} %pad_maximum_fusion.1), calls=%async_computation.1 | async-start | bytes 524288 | tf_op jit(solution)/shard_map/all_to_all | solution.py:179
  21.8 1.4 copy.15
  23.1 0.1 copy.16
  23.2 0.3 copy.17
  23.5 9.4 %all-to-all-done.1 = f32[32,16,128]{2,1,0:T(8,128)S(1)} async-done(((f32[32,16,128]{2,1,0:T(8,128)}), f32[32,16,128]{2,1,0:T(8,128)S(1)}, u32[]{:S(2)}, u32[]{:S(2)}) %all-to-all-start.1) | async-done | bytes 262176 | tf_op jit(solution)/shard_map/all_to_all | solution.py:179
  33.0 1.1 broadcast_in_dim.11
  34.1 3.6 %all-to-all-start = ((f32[8,64,512]{2,1,0:T(8,128)}), f32[8,64,512]{2,1,0:T(8,128)S(1)}, u32[]{:S(2)}, u32[]{:S(2)}) async-start(f32[8,64,512]{2,1,0:T(8,128)} %bitcast.4), calls=%async_computation | async-start | bytes 2097152 | tf_op jit(solution)/shard_map/all_to_all | solution.py:172
  37.7 0.0 copy-done
  37.7 0.1 split_ahead.3
  37.9 27.2 %all-to-all-done.a_ref = f32[8,64,512]{2,1,0:T(8,128)S(1)} async-done(((f32[8,64,512]{2,1,0:T(8,128)}), f32[8,64,512]{2,1,0:T(8,128)S(1)}, u32[]{:S(2)}, u32[]{:S(2)}) %all-to-all-start) | async-done | bytes 1048608 | tf_op jit(solution)/shard_map/all_to_all | solution.py:172
  65.1 0.1 split_ahead.2
  65.2 8.8 %all-gather.3.cloned.1.call-done = f32[1024,2048]{1,0:T(8,128)} async-done(((f32[64,2048]{1,0:T(8,128)}), f32[1024,2048]{1,0:T(8,128)}) %all-gather.3.cloned.1.call-update) | async-done | bytes 8388624 | tf_op jit(solution)/shard_map/all_gather | solution.py:184
  74.0 7.8 %solve.1 = (f32[1024,256]{1,0:T(8,128)}, f32[8,256,128]{2,1,0:T(8,128)}) custom-call(f32[16,64,2048]{2,1,0:T(8,128)} %bitcast.21, bf16[1024,256]{1,0:T(8,128)(2,1)S(1)} %get-tuple-element.20.r_hi, bf16[1024,256]{1,0:T(8,128)(2,1)S(1)} %get-tuple-element.21.r_lo), custom_call_target="tpu_custom_call" | custom-call | tf_op jit(solution)/shard_map/solve/pallas_call | solution.py:84
  81.8 20.0 %all_to_all.30.parts_ref = f32[8,256,128]{2,1,0:T(8,128)S(1)} all-to-all(f32[8,256,128]{2,1,0:T(8,128)} %get-tuple-element.27), channel_id=1, replica_groups=mesh['ya'=4,'yb'=2,'x'=4,'z'=8,'c'=2] {'yb','x'}, dimensions={0} | all-to-all | bytes 2097152 | tf_op jit(solution)/shard_map/all_to_all | solution.py:190
  101.8 1.0 collect.1
  102.8 16.4 %all_to_all.31 = f32[4,128,128]{2,1,0:T(8,128)S(1)} all-to-all(f32[4,128,128]{2,1,0:T(8,128)S(1)} %collect.1), channel_id=1, replica_groups=mesh['ya'=4,'yb'=2,'x'=4,'z'=8,'c'=2] {'ya'}, dimensions={0} | all-to-all | bytes 524288 | tf_op jit(solution)/shard_map/all_to_all | solution.py:191
  119.2 9.0 %all_to_all.32.column_ref = f32[4,128,128]{2,1,0:T(8,128)S(1)} all-to-all(f32[4,128,128]{2,1,0:T(8,128)S(1)} %broadcast_in_dim.14), channel_id=1, replica_groups=mesh['ya'=4,'yb'=2,'x'=4,'z'=8,'c'=2] {'x'}, dimensions={0} | all-to-all | bytes 524288 | tf_op jit(solution)/shard_map/all_to_all | solution.py:193
  128.2 0.6 root.1
  128.8 13.5 %all_to_all.33 = f32[8,64,128]{2,1,0:T(8,128)S(1)} all-to-all(f32[8,64,128]{2,1,0:T(8,128)S(1)} %root.1), channel_id=1, replica_groups=mesh['ya'=4,'yb'=2,'x'=4,'z'=8,'c'=2] {'ya','yb'}, dimensions={0} | all-to-all | bytes 524288 | tf_op jit(solution)/shard_map/all_to_all | solution.py:194
  142.3 0.6 pad_maximum_fusion.2
  (12 shorter events, 0.1 us)
Async XLA Ops:
  7.2 30.5 %copy-start = (f32[1024,256]{1,0:T(8,128)S(1)}, f32[1024,256]{1,0:T(8,128)}, u32[]{:S(2)}) copy-start(f32[1024,256]{1,0:T(8,128)} %a_ref.1) | copy-start | bytes 3145732
  7.2 66.9 %all-gather.3.cloned.1.call-start = ((), (), s32[]{:S(2)}) async-start(), calls=%async_computation.6 | async-start | bytes 8912896 | tf_op jit(solution)/shard_map/all_gather | solution.py:184
  11.5 21.5 %all-to-all-start.1 = ((f32[32,16,128]{2,1,0:T(8,128)}), f32[32,16,128]{2,1,0:T(8,128)S(1)}, u32[]{:S(2)}, u32[]{:S(2)}) async-start(f32[32,16,128]{2,1,0:T(8,128)} %pad_maximum_fusion.1), calls=%async_computation.1 | async-start | bytes 524288 | tf_op jit(solution)/shard_map/all_to_all | solution.py:179
  34.1 31.0 %all-to-all-start = ((f32[8,64,512]{2,1,0:T(8,128)}), f32[8,64,512]{2,1,0:T(8,128)S(1)}, u32[]{:S(2)}, u32[]{:S(2)}) async-start(f32[8,64,512]{2,1,0:T(8,128)} %bitcast.4), calls=%async_computation | async-start | bytes 2097152 | tf_op jit(solution)/shard_map/all_to_all | solution.py:172
Sparse Core Ops, SparseCore 0:
  10.1 63.9 all-gather.2
